TPU v7x, 512 devices: a whole 4x8x8 slice. The times are simulated.
512 devices in a mesh: dp: 16 (over x, y_hi), dom: 32 (over z, y_lo, core).
Axes of the slice: x: 4, y: 8 (y_hi: 4, y_lo: 2; y = y_hi * 2 + y_lo), z: 8, core: 2. Of those that a mesh axis runs over, the one named last changes fastest.
Arguments:
- features: bfloat16 [16, 16384, 128], P('dp', 'dom'), may hold values from -6 to 6
- keep_masks: bfloat16 [16, 4, 16384], P('dp', None, 'dom'), may hold values from 0 to 1, as said below
- serve_ids: int32 [16, 32, 32, 1], P('dp', 'dom'), may hold values from 0 to 3, as said below
- col_slot: int32 [16, 128, 10], P('dp', 'dom'), may hold values from 0 to 35, as said below
- adj_blocks: bfloat16 [16, 128, 10, 128, 128], P('dp', 'dom'), may hold values from -0.15625 to 0.15625
- node_labels: int32 [16, 16384], P('dp', 'dom'), may hold values from 0 to 171
- labeled: int32 [16, 16384], P('dp', 'dom'), may hold values 0 or 1
- weight_in: bfloat16 [128, 1024], replicated, may hold values from -0.5 to 0.5
- bias_in: float32 [1024], replicated, may hold values from -3 to 3
- weight_out: bfloat16 [1024, 172], replicated, may hold values from -0.1875 to 0.1875
- bias_out: float32 [172], replicated, may hold values from -4 to 4
Outputs:
- grad_weight_in: float32 [128, 1024], replicated
- grad_bias_in: float32 [1024], replicated
- grad_weight_out: float32 [1024, 172], replicated
- grad_bias_out: float32 [172], replicated
Inputs may be any that keep to these rules, and one draw needn't show every extreme that they name: `serve_ids`: for each batch, sending device and receiving device: 1 distinct own tile numbers of the sender. `col_slot`: slots below 32 name received tiles; within one device's row tiles every such slot is named exactly once and each own tile slot exactly 2 times. `keep_masks`: values are 0 or 1.
All inputs are finite; a program needn't handle non-finite values. No bound on the sum of `labeled` on one device may be relied on, other than what follows from the above.
Results may differ from a plain program's by a relative error of at most 0.0015.
Values may be sent and summed in bfloat16 or wider, within the bound.
A program may use at most 64 MiB of HBM per device.

v0:
```python
import jax
import jax.numpy as jnp
from jax import lax
from jax.sharding import PartitionSpec as P

ORDER = 2


KEEP_RATE = 0.5


def tile_products(block_vals, picked):
    return jnp.einsum("rjab,rjsbf->rsaf", block_vals, picked, preferred_element_type=jnp.float32)


def mlp_grads(xbar, node_labels, labeled, weight_in, bias_in, weight_out, bias_out, scale):
    row_tiles, samples, tile_size, feat_size = xbar.shape
    classes = weight_out.shape[1]
    node_rows = xbar.reshape(-1, feat_size)
    hidden_pre = jnp.dot(node_rows, weight_in, preferred_element_type=jnp.float32) + bias_in
    activation = jax.nn.silu(hidden_pre).astype(jnp.bfloat16)
    logits = jnp.dot(activation, weight_out, preferred_element_type=jnp.float32) + bias_out
    expo = jnp.exp(logits)
    prob = (expo / jnp.sum(expo, -1, keepdims=True)).reshape(row_tiles, samples, tile_size, classes)
    average = jnp.mean(prob, axis=1)
    squares = average * average
    sharp = squares / jnp.sum(squares, -1, keepdims=True)
    onehot = (
        node_labels.reshape(row_tiles, tile_size)[..., None] == jnp.arange(classes, dtype=jnp.int32)
    ).astype(jnp.float32)
    used = labeled.reshape(row_tiles, 1, tile_size, 1).astype(jnp.float32)
    push = 2.0 * (prob - sharp[:, None])
    inner = jnp.sum(push * prob, -1, keepdims=True)
    dlogits = (used * (prob - onehot[:, None]) + prob * (push - inner)) * scale
    dlogits = dlogits.reshape(-1, classes)
    dlog_b = dlogits.astype(jnp.bfloat16)
    grad_weight_out = jnp.dot(activation.T, dlog_b, preferred_element_type=jnp.float32)
    grad_bias_out = jnp.sum(dlogits, 0)
    dact = jnp.dot(dlog_b, weight_out.T, preferred_element_type=jnp.float32)
    sigma = jax.nn.sigmoid(hidden_pre)
    dpre = dact * sigma * (1.0 + hidden_pre * (1.0 - sigma))
    grad_bias_in = jnp.sum(dpre, 0)
    grad_weight_in = jnp.dot(
        node_rows.T, dpre.astype(jnp.bfloat16), preferred_element_type=jnp.float32
    )
    return (grad_weight_in, grad_bias_in, grad_weight_out, grad_bias_out)


def per_device(
    features,
    keep_masks,
    serve_ids,
    col_slot,
    adj_blocks,
    node_labels,
    labeled,
    weight_in,
    bias_in,
    weight_out,
    bias_out,
):
    tiles_dev = col_slot.shape[1]
    tile_size = adj_blocks.shape[-1]
    feat_size = features.shape[-1]
    samples = keep_masks.shape[1]
    dom_count = lax.axis_size("dom")
    capacity = serve_ids.shape[-1]
    send_ids = serve_ids[0, 0].reshape(-1)
    slot_ids = col_slot[0]
    block_vals = adj_blocks[0]
    own_tiles = features[0].reshape(tiles_dev, tile_size, feat_size)
    mask_tiles = keep_masks[0].reshape(samples, tiles_dev, tile_size).transpose(1, 0, 2)
    masked = mask_tiles[:, :, :, None] * own_tiles[:, None, :, :]
    outgoing = masked[send_ids].reshape(dom_count, capacity, samples, tile_size, feat_size)
    incoming = lax.all_to_all(outgoing, "dom", split_axis=0, concat_axis=0, tiled=True)
    pool = jnp.concatenate([incoming.reshape(-1, samples, tile_size, feat_size), masked], 0)
    picked = pool[slot_ids]
    result = tile_products(block_vals, picked)
    total = masked.astype(jnp.float32) + result
    current = result.astype(jnp.bfloat16)
    outgoing = current[send_ids].reshape(dom_count, capacity, samples, tile_size, feat_size)
    incoming = lax.all_to_all(outgoing, "dom", split_axis=0, concat_axis=0, tiled=True)
    pool = jnp.concatenate([incoming.reshape(-1, samples, tile_size, feat_size), current], 0)
    result = tile_products(block_vals, pool[slot_ids])
    total = total + result
    xbar = (total * (1.0 / ((ORDER + 1) * KEEP_RATE))).astype(jnp.bfloat16)
    scale = 1.0 / (samples * tiles_dev * tile_size)
    grad_w1, grad_b1, grad_w2, grad_b2 = mlp_grads(
        xbar, node_labels[0], labeled[0], weight_in, bias_in, weight_out, bias_out, scale
    )
    grad_w1, grad_b1, grad_w2, grad_b2 = lax.psum(
        (grad_w1, grad_b1, grad_w2, grad_b2), ("dp", "dom")
    )
    return (grad_w1, grad_b1, grad_w2, grad_b2)


def solution(mesh):
    placed = (
        P("dp", "dom", None),
        P("dp", None, "dom"),
        P("dp", "dom", None, None),
        P("dp", "dom", None),
        P("dp", "dom", None, None, None),
        P("dp", "dom"),
        P("dp", "dom"),
        P(),
        P(),
        P(),
        P(),
    )
    return jax.shard_map(
        per_device, mesh=mesh, in_specs=placed, out_specs=(P(), P(), P(), P()), check_vma=False
    )
```

profile of v0, /device:TPU:1, one launch (start us, length us, event | category | flops | bytes accessed | tf_op | source)
XLA Modules:
  0.0 595.2 jit_solution(16002134750879423810)
XLA Ops:
  7.2 0.0 copy-start
  7.2 0.8 fusion.20
  8.0 1.2 broadcast_multiply_fusion
  9.2 3.1 gather_fusion
  12.3 13.2 %all-to-all-start = ((bf16[32,1,4,128,128]{4,3,2,1,0:T(8,128)(2,1)}), bf16[32,1,4,128,128]{4,3,2,1,0:T(8,128)(2,1)}, u32[]{:S(2)}, u32[]{:S(2)}) async-start(bf16[32,1,4,128,128]{4,3,2,1,0:T(8,128)(2,1)} %bitcast.86), calls=%async_computation | async-start | bytes 8388608 | tf_op jit(solution)/shard_map/all_to_all | solution.py:75
  25.4 0.0 copy-done.6
  25.5 0.1 reshape.132
  25.5 101.8 %all-to-all-done = bf16[32,1,4,128,128]{4,3,2,1,0:T(8,128)(2,1)} async-done(((bf16[32,1,4,128,128]{4,3,2,1,0:T(8,128)(2,1)}), bf16[32,1,4,128,128]{4,3,2,1,0:T(8,128)(2,1)}, u32[]{:S(2)}, u32[]{:S(2)}) %all-to-all-start) | async-done | bytes 4194336 | tf_op jit(solution)/shard_map/all_to_all | solution.py:75
  127.3 4.8 pad_maximum_fusion
  132.1 6.9 %gather_fusion.1 = bf16[40,4,128,128]{3,2,1,0:T(8,128)(2,1)} fusion(bf16[36,4,128,128]{3,2,1,0:T(8,128)(2,1)} %pad_maximum_fusion, s32[1024]{0:T(1024)S(1)} %pad_clamp_fusion), kind=kCustom, calls=%fused_computation.1 | custom fusion | bytes 10485920 | tf_op jit(solution)/shard_map/gather | solution.py:77
  139.0 0.0 copy-done
  139.0 4.4 fusion.22
  143.5 3.1 gather_fusion.2
  146.5 9.6 %all-to-all-start.1 = ((bf16[32,1,4,128,128]{4,3,2,1,0:T(8,128)(2,1)}), bf16[32,1,4,128,128]{4,3,2,1,0:T(8,128)(2,1)}, u32[]{:S(2)}, u32[]{:S(2)}) async-start(bf16[32,1,4,128,128]{4,3,2,1,0:T(8,128)(2,1)} %bitcast.85), calls=%async_computation.1 | async-start | bytes 8388608 | tf_op jit(solution)/shard_map/all_to_all | solution.py:82
  156.2 0.0 all-reduce.4.cloned.1.call-start
  156.2 0.0 copy-done.7
  156.3 0.1 fusion.17
  156.4 0.2 sub.35
  156.6 1.7 sub.36
  158.3 99.8 %all-to-all-done.1 = bf16[32,1,4,128,128]{4,3,2,1,0:T(8,128)(2,1)} async-done(((bf16[32,1,4,128,128]{4,3,2,1,0:T(8,128)(2,1)}), bf16[32,1,4,128,128]{4,3,2,1,0:T(8,128)(2,1)}, u32[]{:S(2)}, u32[]{:S(2)}) %all-to-all-start.1) | async-done | bytes 4194336 | tf_op jit(solution)/shard_map/all_to_all | solution.py:82
  258.1 4.8 pad_maximum_fusion.1
  262.9 7.2 %gather_fusion.3 = bf16[40,4,128,128]{3,2,1,0:T(8,128)(2,1)} fusion(bf16[36,4,128,128]{3,2,1,0:T(8,128)(2,1)} %pad_maximum_fusion.1, s32[1024]{0:T(1024)S(1)} %pad_clamp_fusion), kind=kCustom, calls=%fused_computation.3 | custom fusion | bytes 10485920 | tf_op jit(solution)/shard_map/gather | solution.py:84
  270.1 0.0 copy-done.3
  270.1 3.6 fusion.11
  273.7 0.0 copy-start.8
  273.7 0.0 copy-start.11
  273.7 4.6 multiply_convert_fusion
  278.3 1.6 fusion.23
  280.0 0.3 copy-done.12
  280.3 1.3 broadcast_divide_fusion
  281.6 3.0 reshape.121
  284.6 2.3 reduce_sum.55
  286.9 0.2 fusion.19
  287.1 0.1 fusion.18
  287.2 1.3 sub.38
  288.5 2.8 sub.39
  291.3 1.8 multiply_reduce_fusion
  293.1 2.5 fusion.21
  295.5 1.8 fusion.14
  297.3 6.5 %fusion.24 = (f32[1024]{0:T(1024)S(1)}, bf16[2048,1024]{1,0:T(8,128)(2,1)S(1)}) fusion(f32[2048,1024]{1,0:T(8,128)} %get-tuple-element.13, f32[1024]{0:T(1024)S(1)} %copy-done.10, bf16[1024,172]{0,1:T(8,128)(2,1)S(1)} %copy-done.8, bf16[2048,172]{0,1:T(8,128)(2,1)S(1)} %get-tuple-element.9), kind=kOutput, calls=%fused_computation.41 | convolution fusion | flops 744487936 | bytes 13647872 | tf_op jit(solution)/shard_map/dot_general | solution.py:39
  303.8 0.0 copy-start.1
  303.8 1.6 fusion
  305.4 0.0 all-reduce.4.cloned.1.call-update
  305.4 102.3 %all-reduce = (f32[1024]{0:T(1024)}, f32[172]{0:T(256)}) all-reduce(f32[1024]{0:T(1024)S(1)} %get-tuple-element.16, f32[172]{0:T(256)S(1)} %get-tuple-element.8), channel_id=1, replica_groups=mesh['dp'=16,'dom'=32] {'dp','dom'}, use_global_device_ids=true, to_apply=%region_6.7 | all-reduce | flops 1196 | bytes 9568 | tf_op jit(solution)/shard_map/psum | solution.py:91
  407.7 176.7 %all-reduce.4.cloned.1.call-done = (f32[128,1024]{1,0:T(8,128)}, f32[1024,172]{0,1:T(8,128)}) async-done(((f32[128,1024]{1,0:T(8,128)}, f32[1024,172]{0,1:T(8,128)}), (f32[128,1024]{1,0:T(8,128)}, f32[1024,172]{0,1:T(8,128)})) %all-reduce.4.cloned.1.call-update) | async-done | bytes 1228816 | tf_op jit(solution)/shard_map/psum | solution.py:91
  584.4 1.9 copy.28
  586.3 2.0 copy.29
  588.3 0.0 copy-done.1
  (23 shorter events, 0.1 us)
Async XLA Ops:
  7.2 131.9 %copy-start = (bf16[1,4,10,128,128]{4,3,2,1,0:T(8,128)(2,1)S(1)}, bf16[1,4,10,128,128]{4,3,2,1,0:T(8,128)(2,1)}, u32[]{:S(2)}) copy-start(bf16[1,4,10,128,128]{4,3,2,1,0:T(8,128)(2,1)} %param.15) | copy-start | bytes 3932164
  12.3 13.2 %copy-start.6 = (s32[1,4,10]{2,1,0:T(4,128)S(1)}, s32[1,4,10]{2,1,0:T(4,128)}, u32[]{:S(2)}) copy-start(s32[1,4,10]{2,1,0:T(4,128)} %param.14) | copy-start | bytes 484
  12.3 115.1 %all-to-all-start = ((bf16[32,1,4,128,128]{4,3,2,1,0:T(8,128)(2,1)}), bf16[32,1,4,128,128]{4,3,2,1,0:T(8,128)(2,1)}, u32[]{:S(2)}, u32[]{:S(2)}) async-start(bf16[32,1,4,128,128]{4,3,2,1,0:T(8,128)(2,1)} %bitcast.86), calls=%async_computation | async-start | bytes 8388608 | tf_op jit(solution)/shard_map/all_to_all | solution.py:75
  146.5 9.7 %copy-start.7 = (s32[1,512]{1,0:T(1,128)S(1)}, s32[1,512]{1,0:T(1,128)}, u32[]{:S(2)}) copy-start(s32[1,512]{1,0:T(1,128)} %param.17) | copy-start | bytes 6148
  146.5 9.7 %copy-start.5 = (s32[1,512]{1,0:T(1,128)S(1)}, s32[1,512]{1,0:T(1,128)}, u32[]{:S(2)}) copy-start(s32[1,512]{1,0:T(1,128)} %param.16) | copy-start | bytes 6148
  146.5 111.6 %all-to-all-start.1 = ((bf16[32,1,4,128,128]{4,3,2,1,0:T(8,128)(2,1)}), bf16[32,1,4,128,128]{4,3,2,1,0:T(8,128)(2,1)}, u32[]{:S(2)}, u32[]{:S(2)}) async-start(bf16[32,1,4,128,128]{4,3,2,1,0:T(8,128)(2,1)} %bitcast.85), calls=%async_computation.1 | async-start | bytes 8388608 | tf_op jit(solution)/shard_map/all_to_all | solution.py:82
  156.2 428.2 %all-reduce.4.cloned.1.call-start = ((), (), s32[]{:S(2)}) async-start(), calls=%async_computation.2 | async-start | bytes 2490368 | tf_op jit(solution)/shard_map/psum | solution.py:91
  262.9 7.2 %copy-start.2 = (f32[4,4,128,128]{3,2,1,0:T(8,128)S(1)}, f32[4,4,128,128]{3,2,1,0:T(8,128)}, u32[]{:S(2)}) copy-start(f32[4,4,128,128]{3,2,1,0:T(8,128)} %get-tuple-element.11) | copy-start | bytes 3145732
  262.9 7.2 %copy-start.3 = (bf16[1,512,128]{2,1,0:T(8,128)(2,1)S(1)}, bf16[1,512,128]{2,1,0:T(8,128)(2,1)}, u32[]{:S(2)}) copy-start(bf16[1,512,128]{2,1,0:T(8,128)(2,1)} %param.11) | copy-start | bytes 393220
  262.9 7.2 %copy-start.4 = (bf16[1,4,512]{2,1,0:T(4,128)(2,1)S(1)}, bf16[1,4,512]{2,1,0:T(4,128)(2,1)}, u32[]{:S(2)}) copy-start(bf16[1,4,512]{2,1,0:T(4,128)(2,1)} %param.12) | copy-start | bytes 12292
  270.1 3.6 copy-start.9
  270.1 3.6 copy-start.10
  273.7 4.7 copy-start.8
  273.7 4.6 copy-start.11
  278.3 2.0 copy-start.12
  291.3 4.3 copy-start.13
  303.8 284.5 %copy-start.1 = (bf16[1,4,10,128,128]{4,3,2,1,0:T(8,128)(2,1)S(1)}, bf16[1,4,10,128,128]{4,3,2,1,0:T(8,128)(2,1)}, u32[]{:S(2)}) copy-start(bf16[1,4,10,128,128]{4,3,2,1,0:T(8,128)(2,1)} %param.15) | copy-start | bytes 3932164
Sparse Core Ops, SparseCore 0:
  305.5 278.8 all-reduce.3
where the time goes:
time: 596 us; the launch traced here: 595 us
  waiting for transfers between devices  378 us (63%)
  blocking collectives  102 us (17%)
  local copies, waits for them, and re-layouts  33.7 us (6%)
  matrix products  24 us (4%)
  starting transfers between devices  22.9 us (4%)
  other arithmetic  19.7 us (3%)
  between operations  14.2 us (2%)
    all_to_all x2, waiting for transfers between devices, per_device(): lax.all_to_all(outgoing, 'dom', split_axis=0, concat_axis=0, tiled=True)  202 us
    psum x1, waiting for transfers between devices, per_device(): lax.psum((grad_w1, grad_b1, grad_w2, grad_b2), ('dp', 'dom'))  177 us
    psum x1, blocking collectives, per_device(): lax.psum((grad_w1, grad_b1, grad_w2, grad_b2), ('dp', 'dom'))  102 us
    all_to_all x2, starting transfers between devices, per_device(): lax.all_to_all(outgoing, 'dom', split_axis=0, concat_axis=0, tiled=True)  22.8 us
  transfers between devices with their start and end apart: 3, of which 3 were waited for; matrix products, arithmetic and copies ran while one was open for 0% of the time, Pallas kernels for 0%

commit v1 on v0

v1 whole, which is shorter than its diff:
```python
import functools

import jax
import jax.numpy as jnp
from jax import lax
from jax.experimental import pallas as pl
from jax.experimental.pallas import tpu as pltpu
from jax.sharding import PartitionSpec as P

ORDER = 2
KEEP_RATE = 0.5
GROWS = 320
MESH = pl.DeviceIdType.MESH


def place(x, y, z, c):
    return (x * 4 + lax.div(y, 2), z * 4 + lax.rem(y, 2) * 2 + c)


def my_place():
    dp = lax.axis_index("dp")
    dom = lax.axis_index("dom")
    x = lax.div(dp, 4)
    y = lax.rem(dp, 4) * 2 + lax.rem(lax.div(dom, 2), 2)
    z = lax.div(dom, 4)
    c = lax.rem(dom, 2)
    return x, y, z, c


def all_reduce_kernel(
    g_ref, o_ref, core_in, held, first_in, second, second_in, third, third_in, fourth,
    core_s, core_r, one_s, one_r, two_s, two_r, three_s, three_r,
    four_s, four_r, five_s, five_r, six_s, six_r,
):
    x, y, z, c = my_place()
    other = lax.rem(c + 1, 2)
    partner = place(x, y, z, other)
    mine = (z, y)

    def along(axis, d):
        if axis == 0:
            k = lax.rem(z + d, 8)
            return k, place(x, y, k, c)
        k = lax.rem(y + d, 8)
        return k, place(x, k, z, c)

    def remote(src, dst, send_sem, recv_sem, target):
        return pltpu.make_async_remote_copy(
            src_ref=src, dst_ref=dst, send_sem=send_sem, recv_sem=recv_sem,
            device_id=target, device_id_type=MESH,
        )

    def each(start, stop, body):
        def step(i, carry):
            body(i)
            return carry

        lax.fori_loop(start, stop, step, 0)

    barrier = pltpu.get_barrier_semaphore()
    pl.semaphore_signal(barrier, inc=1, device_id=partner, device_id_type=MESH)

    def greet(d):
        for axis in range(2):
            pl.semaphore_signal(barrier, inc=1, device_id=along(axis, d)[1], device_id_type=MESH)

    def greet_x(d):
        target = place(lax.rem(x + d, 4), y, z, c)
        pl.semaphore_signal(barrier, inc=1, device_id=target, device_id_type=MESH)

    each(1, 8, greet)
    each(1, 4, greet_x)
    second[...] = jnp.zeros_like(second)
    pl.semaphore_wait(barrier, 18)

    def core_copy(half, d):
        k = lax.rem(mine[half] + d, 8)
        return remote(
            g_ref.at[other, half, k], core_in.at[half, k],
            core_s.at[half, d], core_r.at[half, d], partner,
        )

    def core_start(i):
        for half in range(2):
            core_copy(half, lax.rem(i, 8)).start()

    each(1, 9, core_start)

    def one_copy(half, d):
        k, target = along(half, d)
        return remote(
            held.at[half, k], first_in.at[half, d - 1],
            one_s.at[half, d - 1], one_r.at[half, d - 1], target,
        )

    def core_add(i):
        d = lax.rem(i, 8)
        for half in range(2):
            k = lax.rem(mine[half] + d, 8)
            core_copy(half, d).wait_recv()
            held[half, k] = g_ref[c, half, k] + core_in[half, k]

    def one_step(d):
        core_add(d)
        for half in range(2):
            one_copy(half, d).start()

    each(1, 8, one_step)
    core_add(8)

    def one_wait(d):
        for half in range(2):
            one_copy(half, d).wait_recv()

    each(1, 8, one_wait)
    for half in range(2):
        total = held[half, mine[half]]
        for d in range(7):
            total = total + first_in[half, d]
        second[half, pl.ds(0, 5)] = total

    def two_copy(half, d):
        k, target = along(1 - half, d)
        return remote(
            second.at[half, k], second_in.at[half, d - 1],
            two_s.at[half, d - 1], two_r.at[half, d - 1], target,
        )

    def two_step(d):
        for half in range(2):
            two_copy(half, d).start()

    def two_wait(d):
        for half in range(2):
            two_copy(half, d).wait_recv()

    each(1, 8, two_step)
    each(1, 8, two_wait)
    for half in range(2):
        total = second[half, mine[1 - half]]
        for d in range(7):
            total = total + second_in[half, d]
        third[half] = total

    def three_copy(d):
        target = place(lax.rem(x + d, 4), y, z, c)
        return remote(third, third_in.at[x], three_s.at[d - 1], three_r.at[d - 1], target)

    each(1, 4, lambda d: three_copy(d).start())
    third_in[x] = third[...]
    each(1, 4, lambda d: three_copy(d).wait_recv())
    total = (third_in[0] + third_in[1]) + (third_in[2] + third_in[3])
    for half in range(2):
        fourth[half, mine[1 - half]] = total[half]

    def four_copy(half, d):
        target = along(1 - half, d)[1]
        piece = fourth.at[half, mine[1 - half]]
        return remote(piece, piece, four_s.at[half, d - 1], four_r.at[half, d - 1], target)

    def four_step(d):
        for half in range(2):
            four_copy(half, d).start()

    def four_wait(d):
        for half in range(2):
            four_copy(half, d).wait_recv()

    each(1, 8, four_step)
    each(1, 8, four_wait)

    def five_copy(half, d):
        target = along(half, d)[1]
        return remote(
            fourth.at[half, pl.ds(0, 5)], o_ref.at[c, half, mine[half]],
            five_s.at[half, d - 1], five_r.at[half, d - 1], target,
        )

    def five_step(d):
        for half in range(2):
            five_copy(half, d).start()

    each(1, 8, five_step)

    def six_copy(half, d):
        k = lax.rem(mine[half] + 8 - d, 8)
        piece = o_ref.at[c, half, k]
        return remote(piece, piece, six_s.at[half, d - 1], six_r.at[half, d - 1], partner)

    def six_own(half):
        return remote(
            fourth.at[half, pl.ds(0, 5)], o_ref.at[c, half, mine[half]],
            six_s.at[half, 7], six_r.at[half, 7], partner,
        )

    for half in range(2):
        six_own(half).start()
        o_ref[c, half, mine[half]] = fourth[half, pl.ds(0, 5)]

    def six_step(d):
        for half in range(2):
            five_copy(half, d).wait_recv()
            six_copy(half, d).start()

    each(1, 8, six_step)

    def finish(d):
        for half in range(2):
            one_copy(half, d).wait_send()
            two_copy(half, d).wait_send()
            four_copy(half, d).wait_send()
            five_copy(half, d).wait_send()
            six_copy(half, d).wait_send()
            six_copy(half, d).wait_recv()

    def finish_core(d):
        for half in range(2):
            core_copy(half, d).wait_send()

    each(1, 8, finish)
    each(0, 8, finish_core)
    each(1, 4, lambda d: three_copy(d).wait_send())
    for half in range(2):
        six_own(half).wait_send()
        six_own(half).wait_recv()


def all_reduce(grads):
    piece = (5, 16, 128)
    f32 = jnp.float32
    dma = pltpu.SemaphoreType.DMA
    shape = (2, 2, 8) + piece
    return pl.pallas_call(
        all_reduce_kernel,
        name="all_reduce",
        out_shape=jax.ShapeDtypeStruct(shape, f32),
        in_specs=[pl.BlockSpec(memory_space=pltpu.VMEM)],
        out_specs=pl.BlockSpec(memory_space=pltpu.VMEM),
        scratch_shapes=[
            pltpu.VMEM((2, 8) + piece, f32),
            pltpu.VMEM((2, 8) + piece, f32),
            pltpu.VMEM((2, 7) + piece, f32),
            pltpu.VMEM((2, 8, 16, 128), f32),
            pltpu.VMEM((2, 7, 16, 128), f32),
            pltpu.VMEM((2, 16, 128), f32),
            pltpu.VMEM((4, 2, 16, 128), f32),
            pltpu.VMEM((2, 8, 16, 128), f32),
        ]
        + [dma((2, 8))] * 2
        + [dma((2, 7))] * 4
        + [dma((3,))] * 2
        + [dma((2, 7))] * 4
        + [dma((2, 8))] * 2,
        compiler_params=pltpu.CompilerParams(collective_id=0, has_side_effects=True),
    )(grads.reshape(shape)).reshape(grads.shape)

def exchange_kernel(chunks, own_ids, ids_ref, src_ref, pool_ref, table_v, table_s, staged, *rest):
    ring, rest = rest[: 7 * chunks], rest[7 * chunks :]
    right_s, right_r, left_s, left_r, side_s, side_r, ids_s, ids_r, table_sem = rest
    x, y, z, c = my_place()
    near = lax.rem(y, 2)
    far_y, far_c = y + 1 - 2 * near, 1 - c
    me = z * 4 + near * 2 + c
    right = place(x, y, lax.rem(z + 1, 8), c)
    left = place(x, y, lax.rem(z + 7, 8), c)
    sides = (
        (place(x, y, z, far_c), z * 4 + near * 2 + far_c),
        (place(x, far_y, z, c), z * 4 + (1 - near) * 2 + c),
        (place(x, far_y, z, far_c), z * 4 + (1 - near) * 2 + far_c),
    )
    half = chunks // 2

    def remote(src, dst, send_sem, recv_sem, target):
        return pltpu.make_async_remote_copy(
            src_ref=src, dst_ref=dst, send_sem=send_sem, recv_sem=recv_sem,
            device_id=target, device_id_type=MESH,
        )

    def held(lane, step, q):
        return ring[6 * chunks + q] if step == 4 else ring[(lane * 3 + step - 1) * chunks + q]

    def along(lane, step, q):
        src = src_ref.at[q] if step == 0 else held(lane, step, q)
        sems = ((right_s, right_r), (left_s, left_r))[lane]
        return remote(
            src, held(lane, step + 1, q), sems[0].at[step, q], sems[1].at[step, q],
            (right, left)[lane],
        )

    def ids_copy(d):
        return remote(
            ids_ref, table_v.at[z], ids_s.at[d - 1], ids_r.at[d - 1],
            place(x, y, lax.rem(z + d, 8), c),
        )

    def carried(lane, step, q):
        return step < 3 or (q < half if lane == 0 else q >= half)

    barrier = pltpu.get_barrier_semaphore()
    for d in range(1, 8):
        pl.semaphore_signal(
            barrier, inc=1, device_id=place(x, y, lax.rem(z + d, 8), c), device_id_type=MESH
        )
    for target, _ in sides:
        pl.semaphore_signal(barrier, inc=1, device_id=target, device_id_type=MESH)
    pl.semaphore_wait(barrier, 10)

    for d in range(1, 8):
        ids_copy(d).start()
    for q in range(chunks):
        for lane in range(2):
            along(lane, 0, q).start()

    def side_copy(i, k, q, source):
        return remote(
            staged.at[i, k, q], pool_ref.at[source * 4 + near * 2 + c, q],
            side_s.at[i, k], side_r.at[i, k], sides[k][0],
        )

    def deliver(i, source, block, q, ids):
        for k in range(3):
            staged[i, k, q] = block(ids(sides[k][1]))
        pool_ref[source * 4 + near * 2 + c, q] = block(ids(me))
        for k in range(3):
            side_copy(i, k, q, source).start()

    for q in range(chunks):
        deliver(0, z, lambda t: src_ref[q, t], q, lambda to: own_ids[to])
    for q in range(chunks):
        for t in range(4):
            pool_ref[32 + t, q] = src_ref[q, t]
    table_v[z] = ids_ref[...]
    for d in range(1, 8):
        ids_copy(d).wait_recv()
    local = pltpu.make_async_copy(table_v, table_s, table_sem)
    local.start()
    local.wait()

    for step in range(1, 4):
        for q in range(chunks):
            for lane in range(2):
                along(lane, step - 1, q).wait_recv()
                if carried(lane, step, q):
                    along(lane, step, q).start()
            for lane in range(2):
                source = lax.rem(z + (8 - step if lane == 0 else step), 8)
                block = held(lane, step, q)
                deliver(
                    1 + lane * 3 + step - 1, source, lambda t: block[t], q,
                    lambda to: table_s[source, 0, to],
                )
    source = lax.rem(z + 4, 8)
    for n in range(half):
        for lane in range(2):
            q = n + lane * half
            along(lane, 3, q).wait_recv()
            block = held(0, 4, q)
            deliver(
                7, source, lambda t: block[t], q, lambda to: table_s[source, 0, to]
            )

    for d in range(1, 8):
        ids_copy(d).wait_send()
    for step in range(4):
        for q in range(chunks):
            for lane in range(2):
                if carried(lane, step, q):
                    along(lane, step, q).wait_send()
    for i in range(8):
        for k in range(3):
            whole = remote(
                staged.at[i, k], pool_ref.at[i], side_s.at[i, k], side_r.at[i, k], sides[k][0]
            )
            whole.wait_send()
            whole.wait_recv()


def exchange(own_ids, ids, tiles, collective_id):
    chunks, count, rows, lanes = tiles.shape
    bf16 = tiles.dtype
    dma = pltpu.SemaphoreType.DMA
    vmem = pl.BlockSpec(memory_space=pltpu.VMEM)
    return pl.pallas_call(
        functools.partial(exchange_kernel, chunks),
        name="exchange",
        out_shape=jax.ShapeDtypeStruct((36, chunks, rows, lanes), bf16),
        in_specs=[pl.BlockSpec(memory_space=pltpu.SMEM), vmem, vmem],
        out_specs=vmem,
        scratch_shapes=[
            pltpu.VMEM((8, 8, 128), jnp.int32),
            pltpu.SMEM((8, 8, 128), jnp.int32),
            pltpu.VMEM((8, 3, chunks, rows, lanes), bf16),
        ]
        + [pltpu.VMEM((count, rows, lanes), bf16)] * (7 * chunks)
        + [dma((4, chunks))] * 4
        + [dma((8, 3))] * 2
        + [dma((7,))] * 2
        + [dma(())],
        compiler_params=pltpu.CompilerParams(collective_id=collective_id, has_side_effects=True),
    )(own_ids, ids, tiles)


def tile_and_masks(pool_ref, slot):
    half = 64
    tile = jnp.concatenate([pool_ref[slot, 0, :half], pool_ref[slot, 1, :half]], 0)
    masks = [pool_ref[slot, q, half + i : half + i + 1] for q in range(2) for i in range(2)]
    return tile, masks


def hop_one_kernel(slots_ref, adj_ref, pool_ref, current_ref, base_ref):
    f32 = jnp.float32
    rows = lax.broadcasted_iota(jnp.int32, (128, 128), 0)
    cols = lax.broadcasted_iota(jnp.int32, (128, 128), 1)
    eye = jnp.where(rows == cols, 1.0, 0.0).astype(jnp.bfloat16)

    def row_tile(r, carry):
        own, own_masks = tile_and_masks(pool_ref, 32 + r)
        own_block = jnp.concatenate([eye * m for m in own_masks], 0)
        masked = jnp.dot(own_block, own, preferred_element_type=f32)
        result = jnp.zeros((512, 128), f32)
        for j in range(0, 10, 2):
            blocks, tiles = [], []
            for i in range(2):
                tile, masks = tile_and_masks(pool_ref, slots_ref[r, j + i])
                block = adj_ref[r, j + i]
                blocks.append(jnp.concatenate([block * m for m in masks], 0))
                tiles.append(tile)
            result += jnp.dot(
                jnp.concatenate(blocks, 1), jnp.concatenate(tiles, 0), preferred_element_type=f32
            )
        for s in range(4):
            part = result[s * 128 : (s + 1) * 128]
            current_ref[s, r] = part.astype(jnp.bfloat16)
            base_ref[r, s] = masked[s * 128 : (s + 1) * 128] + part
        return carry

    lax.fori_loop(0, 4, row_tile, 0)


def hop_one(slots, adj, pool):
    vmem = pl.BlockSpec(memory_space=pltpu.VMEM)
    return pl.pallas_call(
        hop_one_kernel,
        name="hop_one",
        out_shape=(
            jax.ShapeDtypeStruct((4, 4, 128, 128), jnp.bfloat16),
            jax.ShapeDtypeStruct((4, 4, 128, 128), jnp.float32),
        ),
        in_specs=[pl.BlockSpec(memory_space=pltpu.SMEM), vmem, vmem],
        out_specs=(vmem, vmem),
    )(slots, adj, pool)


def column(row):
    return jnp.broadcast_to(row, (128, 128)).T[:, :1]


def mlp_kernel(
    slots_ref, adj_ref, pool_ref, base_ref, labels_ref, labeled_ref,
    w_in_ref, b_in_ref, w_out_ref, b_out_ref, g_ref,
    xbar, xbar_t, act, slope, dlog, dlog_t,
):
    f32, bf16 = jnp.float32, jnp.bfloat16
    classes = w_out_ref.shape[0]
    nt = (((1,), (1,)), ((), ()))
    g_ref[...] = jnp.zeros_like(g_ref)

    def row_tile(r, bias_total):
        hop = jnp.zeros((128, 512), f32)
        for j in range(0, 10, 2):
            lhs = jnp.concatenate([adj_ref[r, j], adj_ref[r, j + 1]], 1)
            rhs = jnp.concatenate(
                [
                    jnp.concatenate([pool_ref[slots_ref[r, j + i], s] for s in range(4)], 1)
                    for i in range(2)
                ],
                0,
            )
            hop += jnp.dot(lhs, rhs, preferred_element_type=f32)
        for s in range(4):
            mean = (base_ref[r, s] + hop[:, s * 128 : (s + 1) * 128]) * (
                1.0 / ((ORDER + 1) * KEEP_RATE)
            )
            xbar[r, s * 128 : (s + 1) * 128] = mean.astype(bf16)
            xbar_t[r, :, s * 128 : (s + 1) * 128] = mean.T.astype(bf16)

        rows = xbar[r]
        logits = jnp.zeros((512, classes), f32) + b_out_ref[...]
        for h in range(4):
            cols = slice(h * 256, (h + 1) * 256)
            pre = jnp.dot(rows, w_in_ref[:, cols], preferred_element_type=f32) + b_in_ref[:, cols]
            sigma = 1.0 / (1.0 + jnp.exp(-pre))
            hidden = (pre * sigma).astype(bf16)
            act[h, r] = hidden
            slope[h, r] = sigma * (1.0 + pre * (1.0 - sigma))
            logits += lax.dot_general(hidden, w_out_ref[:, cols], nt, preferred_element_type=f32)

        expo = jnp.exp(logits)
        prob = expo / jnp.sum(expo, -1, keepdims=True)
        parts = [prob[s * 128 : (s + 1) * 128] for s in range(4)]
        average = (parts[0] + parts[1] + parts[2] + parts[3]) * 0.25
        squares = average * average
        sharp = squares / jnp.sum(squares, -1, keepdims=True)
        label = column(labels_ref[pl.ds(r, 1), :].astype(f32)).astype(jnp.int32)
        used = column(labeled_ref[pl.ds(r, 1), :].astype(f32))
        onehot = (label == lax.broadcasted_iota(jnp.int32, (128, classes), 1)).astype(f32)
        for s in range(4):
            push = 2.0 * (parts[s] - sharp)
            inner = jnp.sum(push * parts[s], -1, keepdims=True)
            dlogits = (used * (parts[s] - onehot) + parts[s] * (push - inner)) * (1.0 / 2048.0)
            bias_total = bias_total + jnp.sum(dlogits, 0, keepdims=True)
            dlog[r, s * 128 : (s + 1) * 128] = dlogits.astype(bf16)
            dlog_t[r, :, s * 128 : (s + 1) * 128] = dlogits.T.astype(bf16)
        return bias_total

    bias_total = lax.fori_loop(0, 4, row_tile, jnp.zeros((1, classes), f32))
    g_ref[0, 301:302, :] = bias_total[:, :128]
    g_ref[1, 301:302, : classes - 128] = bias_total[:, 128:]

    for h in range(4):
        cols = slice(h * 256, (h + 1) * 256)

        def back(r, carry):
            w_in_grad, w_out_grad, b_in_grad = carry
            dact = jnp.dot(dlog[r], w_out_ref[:, cols], preferred_element_type=f32)
            dpre = dact * slope[h, r]
            w_in_grad = w_in_grad + jnp.dot(
                xbar_t[r], dpre.astype(bf16), preferred_element_type=f32
            )
            w_out_grad = w_out_grad + jnp.dot(dlog_t[r], act[h, r], preferred_element_type=f32)
            b_in_grad = b_in_grad + jnp.sum(dpre, 0, keepdims=True)
            return w_in_grad, w_out_grad, b_in_grad

        w_in_grad, w_out_grad, b_in_grad = lax.fori_loop(
            0, 4, back,
            (jnp.zeros((128, 256), f32), jnp.zeros((classes, 256), f32), jnp.zeros((1, 256), f32)),
        )
        for i in range(2):
            lanes = slice(i * 128, (i + 1) * 128)
            g_ref[2 * h + i, :128] = w_in_grad[:, lanes]
            g_ref[2 * h + i, 128 : 128 + classes] = w_out_grad[:, lanes]
            g_ref[2 * h + i, 300:301] = b_in_grad[:, lanes]


def mlp(slots, adj, pool, base, labels, labeled, w_in, b_in, w_out_t, b_out):
    vmem = pl.BlockSpec(memory_space=pltpu.VMEM)
    classes = w_out_t.shape[0]
    bf16 = jnp.bfloat16
    return pl.pallas_call(
        mlp_kernel,
        name="mlp",
        out_shape=jax.ShapeDtypeStruct((8, GROWS, 128), jnp.float32),
        in_specs=[pl.BlockSpec(memory_space=pltpu.SMEM)] + [vmem] * 9,
        out_specs=vmem,
        scratch_shapes=[
            pltpu.VMEM((4, 512, 128), bf16),
            pltpu.VMEM((4, 128, 512), bf16),
            pltpu.VMEM((4, 4, 512, 256), bf16),
            pltpu.VMEM((4, 4, 512, 256), jnp.float32),
            pltpu.VMEM((4, 512, classes), bf16),
            pltpu.VMEM((4, classes, 512), bf16),
        ],
    )(slots, adj, pool, base, labels, labeled, w_in, b_in, w_out_t, b_out)


def unpack_kernel(g_ref, w_in_ref, b_in_ref, w_out_ref, b_out_ref):
    classes = w_out_ref.shape[0]
    for i in range(8):
        lanes = slice(i * 128, (i + 1) * 128)
        w_in_ref[:, lanes] = g_ref[i, :128]
        w_out_ref[:, lanes] = g_ref[i, 128 : 128 + classes]
        b_in_ref[:, lanes] = g_ref[i, 300:301]
    b_out_ref[:, :128] = g_ref[0, 301:302]
    b_out_ref[:, 128:] = g_ref[1, 301:302, : classes - 128]


def unpack(summed, classes):
    vmem = pl.BlockSpec(memory_space=pltpu.VMEM)
    shapes = ((128, 1024), (1, 1024), (classes, 1024), (1, classes))
    return pl.pallas_call(
        unpack_kernel,
        name="unpack",
        out_shape=tuple(jax.ShapeDtypeStruct(s, jnp.float32) for s in shapes),
        in_specs=[vmem],
        out_specs=(vmem,) * 4,
    )(summed)


def per_device(
    features, keep_masks, serve_ids, col_slot, adj_blocks, node_labels, labeled,
    weight_in, bias_in, weight_out, bias_out,
):
    classes = weight_out.shape[1]
    own_ids = serve_ids.reshape(-1)
    ids = jnp.pad(own_ids[None], ((0, 7), (0, 96)))
    slots, adj = col_slot[0], adj_blocks[0]
    tiles = features.reshape(4, 2, 64, 128).transpose(1, 0, 2, 3)
    masks = keep_masks.reshape(2, 2, 4, 128).transpose(0, 2, 1, 3)
    both = jnp.concatenate([tiles, jnp.pad(masks, ((0, 0), (0, 0), (0, 6), (0, 0)))], 2)
    pool = exchange(own_ids, ids, both, 1)
    current, base = hop_one(slots, adj, pool)
    pool = exchange(own_ids, ids, current, 2)
    grads = mlp(
        slots, adj, pool, base, node_labels.reshape(4, 128), labeled.reshape(4, 128),
        weight_in, bias_in[None], weight_out.T, bias_out[None],
    )
    w_in, b_in, w_out_t, b_out = unpack(all_reduce(grads), classes)
    return (w_in, b_in[0], w_out_t.T, b_out[0])


def solution(mesh):
    placed = (
        P("dp", "dom", None),
        P("dp", None, "dom"),
        P("dp", "dom", None, None),
        P("dp", "dom", None),
        P("dp", "dom", None, None, None),
        P("dp", "dom"),
        P("dp", "dom"),
        P(),
        P(),
        P(),
        P(),
    )
    return jax.shard_map(
        per_device, mesh=mesh, in_specs=placed, out_specs=(P(), P(), P(), P()), check_vma=False
    )
```

time: 596 us -> 171 us (0.29)
  waiting for transfers between devices: 378 us -> 0 us
  Pallas kernels: 0 us -> 166 us
  blocking collectives: 102 us -> 0 us
  local copies, waits for them, and re-layouts: 33.7 us -> 2.87 us
  matrix products: 24 us -> 0 us
  starting transfers between devices: 22.9 us -> 0 us
  other arithmetic: 19.7 us -> 0.67 us
  between operations: 14.2 us -> 0.66 us
    all_to_all x2 -> x0, waiting for transfers between devices: 202 us -> none  [per_device(): lax.all_to_all(outgoing, 'dom', split_axis=0, concat_axis=0, tiled=True)]
    psum x1 -> x0, waiting for transfers between devices: 177 us -> none  [per_device(): lax.psum((grad_w1, grad_b1, grad_w2, grad_b2), ('dp', 'dom'))]
    pallas_call x0 -> x6, Pallas kernels: none -> 166 us  [the longest x2 91.2 us: exchange(): pl.pallas_call(functools.partial(exchange_kernel, chunks), name='exchange...]
    psum x1 -> x0, blocking collectives: 102 us -> none  [per_device(): lax.psum((grad_w1, grad_b1, grad_w2, grad_b2), ('dp', 'dom'))]
    dot_general x7 -> x0, matrix products: 24 us -> none  [the longest x2 7.99 us: tile_products(): jnp.einsum('rjab,rjsbf->rsaf', block_vals, picked, preferred_element_type...]
    all_to_all x2 -> x0, starting transfers between devices: 22.8 us -> none  [per_device(): lax.all_to_all(outgoing, 'dom', split_axis=0, concat_axis=0, tiled=True)]
    gather x4 -> x0, local copies, waits for them, and re-layouts: 20.2 us -> none  [the longest x1 7.2 us: per_device(): result = tile_products(block_vals, pool[slot_ids])]
    concatenate x2 -> x1, other arithmetic: 9.55 us -> 0.67 us  [per_device(): jnp.concatenate([tiles, jnp.pad(masks, ((0, 0), (0, 0), (0, 6), (0, 0)))]...]
  transfers between devices with their start and end apart: 3 -> 0, of which waited for: 3 -> 0; matrix products, arithmetic and copies ran while one was open for 0% -> 0% of each run, Pallas kernels for 0% -> 0%
where the time goes in v1:
time: 171 us
  Pallas kernels  166 us (97%)
  local copies, waits for them, and re-layouts  2.87 us (2%)
    pallas_call x2, Pallas kernels, exchange(): pl.pallas_call(functools.partial(exchange_kernel, chunks), name='exchange...  91.2 us
    pallas_call x1, Pallas kernels, all_reduce(): pl.pallas_call(all_reduce_kernel, name='all_reduce', out_shape=jax.ShapeD...  47 us
    pallas_call x1, Pallas kernels, mlp(): pl.pallas_call(mlp_kernel, name='mlp', out_shape=jax.ShapeDtypeStruct((8,...  20.5 us
    pallas_call x1, Pallas kernels, hop_one(): pl.pallas_call(hop_one_kernel, name='hop_one', out_shape=(jax.ShapeDtypeS...  5.04 us

profile of v1, /device:TPU:1, one launch (start us, length us, event | category | flops | bytes accessed | tf_op | source)
XLA Modules:
  0.0 170.6 jit_solution(7952075925729743540)
XLA Ops:
  0.6 1.3 pad.8.ids_ref
  1.9 0.7 reshape.31
  2.6 0.9 copy.19
  3.5 0.7 fusion.1.src_ref
  4.2 36.8 %exchange.2.pool_ref = bf16[36,2,72,128]{3,2,1,0:T(8,128)(2,1)} custom-call(s32[32]{0:T(128)} %bitcast.32, s32[8,128]{1,0:T(8,128)} %pad.8.ids_ref, bf16[2,4,72,128]{3,2,1,0:T(8,128)(2,1)} %fusion.1.src_ref), custom_call_target="tpu_custom_call" | custom-call | tf_op jit(solution)/shard_map/exchange/pallas_call | solution.py:383
  41.0 5.0 %hop_one.1 = (bf16[4,4,128,128]{3,2,1,0:T(8,128)(2,1)}, f32[4,4,128,128]{3,2,1,0:T(8,128)}) custom-call(s32[4,10]{1,0:T(4,128)} %bitcast.29, bf16[4,10,128,128]{3,2,1,0:T(8,128)(2,1)} %bitcast.21, bf16[36,2,72,128]{3,2,1,0:T(8,128)(2,1)} %exchange.2.pool_ref), custom_call_target="tpu_custom_call" | custom-call | tf_op jit(solution)/shard_map/hop_one/pallas_call | solution.py:442
  46.1 54.4 %exchange.3.pool_ref = bf16[36,4,128,128]{3,2,1,0:T(8,128)(2,1)} custom-call(s32[32]{0:T(128)} %bitcast.33, s32[8,128]{1,0:T(8,128)} %pad.8.ids_ref, bf16[4,4,128,128]{3,2,1,0:T(8,128)(2,1)} %get-tuple-element.10.src_ref), custom_call_target="tpu_custom_call" | custom-call | tf_op jit(solution)/shard_map/exchange/pallas_call | solution.py:383
  100.5 20.5 %mlp.1 = f32[8,320,128]{2,1,0:T(8,128)} custom-call(s32[4,10]{1,0:T(4,128)} %bitcast.30, bf16[4,10,128,128]{3,2,1,0:T(8,128)(2,1)} %bitcast.22, bf16[36,4,128,128]{3,2,1,0:T(8,128)(2,1)} %exchange.3.pool_ref, f32[4,4,128,128]{3,2,1,0:T(8,128)} %get-tuple-element.11.base_ref, s32[4,128]{1,0:T(4,128)} %bitcast.35, s32[4,128]{1,0:T(4,128)} %bitcast.36, ...), custom_call_target="tpu_custom_call" | custom-call | tf_op jit(solution)/shard_map/mlp/pallas_call | solution.py:549
  121.0 47.0 %all_reduce.1 = f32[2,2,8,5,16,128]{5,4,3,2,1,0:T(8,128)} custom-call(f32[2,2,8,5,16,128]{5,4,3,2,1,0:T(8,128)} %bitcast.23), custom_call_target="tpu_custom_call" | custom-call | tf_op jit(solution)/shard_map/all_reduce/pallas_call | solution.py:233
  168.1 2.5 %unpack.1 = (f32[128,1024]{1,0:T(8,128)}, f32[1,1024]{1,0:T(1,128)}, f32[172,1024]{1,0:T(8,128)}, f32[1,172]{1,0:T(1,128)}) custom-call(f32[8,320,128]{2,1,0:T(8,128)} %bitcast.24), custom_call_target="tpu_custom_call" | custom-call | tf_op jit(solution)/shard_map/unpack/pallas_call | solution.py:580
  (1 shorter events, 0.0 us)

commit v2 on v1

--- a/solution.py
+++ b/solution.py
@@ -1,5 +1,3 @@
-import functools
-
 import jax
 import jax.numpy as jnp
 from jax import lax
@@ -254,47 +252,30 @@
         compiler_params=pltpu.CompilerParams(collective_id=0, has_side_effects=True),
     )(grads.reshape(shape)).reshape(grads.shape)
 
-def exchange_kernel(chunks, own_ids, ids_ref, src_ref, pool_ref, table_v, table_s, staged, *rest):
-    ring, rest = rest[: 7 * chunks], rest[7 * chunks :]
-    right_s, right_r, left_s, left_r, side_s, side_r, ids_s, ids_r, table_sem = rest
+def spread_kernel(
+    own_ids, slots_ref, ids_ref, feat_ref, mask_ref, adj_ref, pool_ref, base_ref,
+    ids_v, table_v, table_s, src, first_pool, current, staged_one, staged_two, *rest,
+):
+    f32, bf16 = jnp.float32, jnp.bfloat16
+    rings = (rest[:14], rest[14:42])
+    sems = (rest[42:48], rest[48:54])
+    ids_s, ids_r, table_sem = rest[54:]
     x, y, z, c = my_place()
     near = lax.rem(y, 2)
     far_y, far_c = y + 1 - 2 * near, 1 - c
     me = z * 4 + near * 2 + c
-    right = place(x, y, lax.rem(z + 1, 8), c)
-    left = place(x, y, lax.rem(z + 7, 8), c)
+    turn = (place(x, y, lax.rem(z + 1, 8), c), place(x, y, lax.rem(z + 7, 8), c))
     sides = (
-        (place(x, y, z, far_c), z * 4 + near * 2 + far_c),
         (place(x, far_y, z, c), z * 4 + (1 - near) * 2 + c),
         (place(x, far_y, z, far_c), z * 4 + (1 - near) * 2 + far_c),
+        (place(x, y, z, far_c), z * 4 + near * 2 + far_c),
     )
-    half = chunks // 2
-
-    def remote(src, dst, send_sem, recv_sem, target):
+
+    def remote(from_ref, to_ref, send_sem, recv_sem, target):
         return pltpu.make_async_remote_copy(
-            src_ref=src, dst_ref=dst, send_sem=send_sem, recv_sem=recv_sem,
+            src_ref=from_ref, dst_ref=to_ref, send_sem=send_sem, recv_sem=recv_sem,
             device_id=target, device_id_type=MESH,
         )
-
-    def held(lane, step, q):
-        return ring[6 * chunks + q] if step == 4 else ring[(lane * 3 + step - 1) * chunks + q]
-
-    def along(lane, step, q):
-        src = src_ref.at[q] if step == 0 else held(lane, step, q)
-        sems = ((right_s, right_r), (left_s, left_r))[lane]
-        return remote(
-            src, held(lane, step + 1, q), sems[0].at[step, q], sems[1].at[step, q],
-            (right, left)[lane],
-        )
-
-    def ids_copy(d):
-        return remote(
-            ids_ref, table_v.at[z], ids_s.at[d - 1], ids_r.at[d - 1],
-            place(x, y, lax.rem(z + d, 8), c),
-        )
-
-    def carried(lane, step, q):
-        return step < 3 or (q < half if lane == 0 else q >= half)
 
     barrier = pltpu.get_barrier_semaphore()
     for d in range(1, 8):
@@ -303,152 +284,197 @@
         )
     for target, _ in sides:
         pl.semaphore_signal(barrier, inc=1, device_id=target, device_id_type=MESH)
+
+    ids_v[...] = jnp.zeros_like(ids_v)
+    ids_v[0:1, 0:32] = ids_ref[...]
+    masks = mask_ref[...].astype(f32)
+    for q in range(2):
+        for t in range(4):
+            begin = t * 128 + q * 64
+            src[q, t, 0:64] = feat_ref[begin : begin + 64]
+            pair = masks[2 * q : 2 * q + 2, t * 128 : (t + 1) * 128]
+            src[q, t, 64:72] = jnp.concatenate([pair, jnp.zeros((6, 128), f32)], 0).astype(bf16)
+            first_pool[32 + t, q] = src[q, t]
     pl.semaphore_wait(barrier, 10)
+
+    def ids_copy(d):
+        return remote(
+            ids_v, table_v.at[z], ids_s.at[d - 1], ids_r.at[d - 1],
+            place(x, y, lax.rem(z + d, 8), c),
+        )
+
+    def learn_ids():
+        table_v[z] = ids_v[...]
+        for d in range(1, 8):
+            ids_copy(d).wait_recv()
+        local = pltpu.make_async_copy(table_v, table_s, table_sem)
+        local.start()
+        local.wait()
+
+    def swap(chunks, src_ref, out, staged, ring, marks, ready, before_others):
+        lane_s, lane_r = marks[0:2], marks[2:4]
+        side_s, side_r = marks[4:6]
+        half = chunks // 2
+
+        def held(lane, step, q):
+            return ring[6 * chunks + q] if step == 4 else ring[(lane * 3 + step - 1) * chunks + q]
+
+        def along(lane, step, q):
+            block = src_ref.at[q] if step == 0 else held(lane, step, q)
+            return remote(
+                block, held(lane, step + 1, q), lane_s[lane].at[step, q],
+                lane_r[lane].at[step, q], turn[lane],
+            )
+
+        def carried(lane, step, q):
+            return step < 3 or (q < half if lane == 0 else q >= half)
+
+        def side_copy(i, k, q, source):
+            return remote(
+                staged.at[i, k, q], out.at[source * 4 + near * 2 + c, q],
+                side_s.at[i, k], side_r.at[i, k], sides[k][0],
+            )
+
+        def deliver(i, source, block, q, ids):
+            for k in range(3):
+                staged[i, k, q] = block(ids(sides[k][1]))
+            out[source * 4 + near * 2 + c, q] = block(ids(me))
+            for k in range(3):
+                side_copy(i, k, q, source).start()
+
+        for q in range(chunks):
+            ready(q)
+            for lane in range(2):
+                along(lane, 0, q).start()
+            deliver(0, z, lambda t: src_ref[q, t], q, lambda to: own_ids[to])
+        before_others()
+        for step in range(1, 4):
+            for q in range(chunks):
+                for lane in range(2):
+                    along(lane, step - 1, q).wait_recv()
+                    if carried(lane, step, q):
+                        along(lane, step, q).start()
+                for lane in range(2):
+                    source = lax.rem(z + (8 - step if lane == 0 else step), 8)
+                    block = held(lane, step, q)
+                    deliver(
+                        1 + lane * 3 + step - 1, source, lambda t: block[t], q,
+                        lambda to: table_s[source, 0, to],
+                    )
+        source = lax.rem(z + 4, 8)
+        for n in range(half):
+            for lane in range(2):
+                q = n + lane * half
+                along(lane, 3, q).wait_recv()
+                block = held(0, 4, q)
+                deliver(7, source, lambda t: block[t], q, lambda to: table_s[source, 0, to])
+        for i in range(8):
+            for k in range(3):
+                remote(
+                    staged.at[i, k], out.at[i], side_s.at[i, k], side_r.at[i, k], sides[k][0]
+                ).wait_recv()
+
+        def finish():
+            for step in range(4):
+                for q in range(chunks):
+                    for lane in range(2):
+                        if carried(lane, step, q):
+                            along(lane, step, q).wait_send()
+            for i in range(8):
+                for k in range(3):
+                    remote(
+                        staged.at[i, k], out.at[i], side_s.at[i, k], side_r.at[i, k], sides[k][0]
+                    ).wait_send()
+
+        return finish
 
     for d in range(1, 8):
         ids_copy(d).start()
-    for q in range(chunks):
-        for lane in range(2):
-            along(lane, 0, q).start()
-
-    def side_copy(i, k, q, source):
-        return remote(
-            staged.at[i, k, q], pool_ref.at[source * 4 + near * 2 + c, q],
-            side_s.at[i, k], side_r.at[i, k], sides[k][0],
-        )
-
-    def deliver(i, source, block, q, ids):
-        for k in range(3):
-            staged[i, k, q] = block(ids(sides[k][1]))
-        pool_ref[source * 4 + near * 2 + c, q] = block(ids(me))
-        for k in range(3):
-            side_copy(i, k, q, source).start()
-
-    for q in range(chunks):
-        deliver(0, z, lambda t: src_ref[q, t], q, lambda to: own_ids[to])
-    for q in range(chunks):
-        for t in range(4):
-            pool_ref[32 + t, q] = src_ref[q, t]
-    table_v[z] = ids_ref[...]
-    for d in range(1, 8):
-        ids_copy(d).wait_recv()
-    local = pltpu.make_async_copy(table_v, table_s, table_sem)
-    local.start()
-    local.wait()
-
-    for step in range(1, 4):
-        for q in range(chunks):
-            for lane in range(2):
-                along(lane, step - 1, q).wait_recv()
-                if carried(lane, step, q):
-                    along(lane, step, q).start()
-            for lane in range(2):
-                source = lax.rem(z + (8 - step if lane == 0 else step), 8)
-                block = held(lane, step, q)
-                deliver(
-                    1 + lane * 3 + step - 1, source, lambda t: block[t], q,
-                    lambda to: table_s[source, 0, to],
+    finish_one = swap(
+        2, src, first_pool, staged_one, rings[0], sems[0], lambda q: None, learn_ids
+    )
+
+    eye = jnp.where(
+        lax.broadcasted_iota(jnp.int32, (128, 128), 0)
+        == lax.broadcasted_iota(jnp.int32, (128, 128), 1),
+        1.0, 0.0,
+    ).astype(bf16)
+
+    def first_hop(s):
+        def tile_and_mask(slot):
+            tile = jnp.concatenate([first_pool[slot, 0, 0:64], first_pool[slot, 1, 0:64]], 0)
+            row = 64 + s % 2
+            return tile, first_pool[slot, s // 2, row : row + 1]
+
+        def row_tile(r, carry):
+            own, mask = tile_and_mask(32 + r)
+            masked = jnp.dot(eye * mask, own, preferred_element_type=f32)
+            result = jnp.zeros((128, 128), f32)
+            for j in range(0, 10, 2):
+                blocks, tiles = [], []
+                for i in range(2):
+                    tile, mask = tile_and_mask(slots_ref[r, j + i])
+                    blocks.append(adj_ref[r, j + i] * mask)
+                    tiles.append(tile)
+                result += jnp.dot(
+                    jnp.concatenate(blocks, 1), jnp.concatenate(tiles, 0),
+                    preferred_element_type=f32,
                 )
-    source = lax.rem(z + 4, 8)
-    for n in range(half):
-        for lane in range(2):
-            q = n + lane * half
-            along(lane, 3, q).wait_recv()
-            block = held(0, 4, q)
-            deliver(
-                7, source, lambda t: block[t], q, lambda to: table_s[source, 0, to]
-            )
-
+            current[s, r] = result.astype(bf16)
+            base_ref[r, s] = masked + result
+            return carry
+
+        lax.fori_loop(0, 4, row_tile, 0)
+
+    def own_tiles():
+        for q in range(4):
+            for t in range(4):
+                pool_ref[32 + t, q] = current[q, t]
+
+    finish_two = swap(
+        4, current, pool_ref, staged_two, rings[1], sems[1], first_hop, own_tiles
+    )
     for d in range(1, 8):
         ids_copy(d).wait_send()
-    for step in range(4):
-        for q in range(chunks):
-            for lane in range(2):
-                if carried(lane, step, q):
-                    along(lane, step, q).wait_send()
-    for i in range(8):
-        for k in range(3):
-            whole = remote(
-                staged.at[i, k], pool_ref.at[i], side_s.at[i, k], side_r.at[i, k], sides[k][0]
-            )
-            whole.wait_send()
-            whole.wait_recv()
-
-
-def exchange(own_ids, ids, tiles, collective_id):
-    chunks, count, rows, lanes = tiles.shape
-    bf16 = tiles.dtype
+    finish_one()
+    finish_two()
+
+
+def spread(own_ids, slots, features, masks, adj):
+    bf16, f32, i32 = jnp.bfloat16, jnp.float32, jnp.int32
     dma = pltpu.SemaphoreType.DMA
     vmem = pl.BlockSpec(memory_space=pltpu.VMEM)
+    smem = pl.BlockSpec(memory_space=pltpu.SMEM)
+
+    def marks(chunks):
+        return [dma((4, chunks))] * 4 + [dma((8, 3))] * 2
+
     return pl.pallas_call(
-        functools.partial(exchange_kernel, chunks),
-        name="exchange",
-        out_shape=jax.ShapeDtypeStruct((36, chunks, rows, lanes), bf16),
-        in_specs=[pl.BlockSpec(memory_space=pltpu.SMEM), vmem, vmem],
-        out_specs=vmem,
+        spread_kernel,
+        name="spread",
+        out_shape=(
+            jax.ShapeDtypeStruct((36, 4, 128, 128), bf16),
+            jax.ShapeDtypeStruct((4, 4, 128, 128), f32),
+        ),
+        in_specs=[smem, smem] + [vmem] * 4,
+        out_specs=(vmem, vmem),
         scratch_shapes=[
-            pltpu.VMEM((8, 8, 128), jnp.int32),
-            pltpu.SMEM((8, 8, 128), jnp.int32),
-            pltpu.VMEM((8, 3, chunks, rows, lanes), bf16),
+            pltpu.VMEM((8, 128), i32),
+            pltpu.VMEM((8, 8, 128), i32),
+            pltpu.SMEM((8, 8, 128), i32),
+            pltpu.VMEM((2, 4, 72, 128), bf16),
+            pltpu.VMEM((36, 2, 72, 128), bf16),
+            pltpu.VMEM((4, 4, 128, 128), bf16),
+            pltpu.VMEM((8, 3, 2, 72, 128), bf16),
+            pltpu.VMEM((8, 3, 4, 128, 128), bf16),
         ]
-        + [pltpu.VMEM((count, rows, lanes), bf16)] * (7 * chunks)
-        + [dma((4, chunks))] * 4
-        + [dma((8, 3))] * 2
-        + [dma((7,))] * 2
-        + [dma(())],
-        compiler_params=pltpu.CompilerParams(collective_id=collective_id, has_side_effects=True),
-    )(own_ids, ids, tiles)
-
-
-def tile_and_masks(pool_ref, slot):
-    half = 64
-    tile = jnp.concatenate([pool_ref[slot, 0, :half], pool_ref[slot, 1, :half]], 0)
-    masks = [pool_ref[slot, q, half + i : half + i + 1] for q in range(2) for i in range(2)]
-    return tile, masks
-
-
-def hop_one_kernel(slots_ref, adj_ref, pool_ref, current_ref, base_ref):
-    f32 = jnp.float32
-    rows = lax.broadcasted_iota(jnp.int32, (128, 128), 0)
-    cols = lax.broadcasted_iota(jnp.int32, (128, 128), 1)
-    eye = jnp.where(rows == cols, 1.0, 0.0).astype(jnp.bfloat16)
-
-    def row_tile(r, carry):
-        own, own_masks = tile_and_masks(pool_ref, 32 + r)
-        own_block = jnp.concatenate([eye * m for m in own_masks], 0)
-        masked = jnp.dot(own_block, own, preferred_element_type=f32)
-        result = jnp.zeros((512, 128), f32)
-        for j in range(0, 10, 2):
-            blocks, tiles = [], []
-            for i in range(2):
-                tile, masks = tile_and_masks(pool_ref, slots_ref[r, j + i])
-                block = adj_ref[r, j + i]
-                blocks.append(jnp.concatenate([block * m for m in masks], 0))
-                tiles.append(tile)
-            result += jnp.dot(
-                jnp.concatenate(blocks, 1), jnp.concatenate(tiles, 0), preferred_element_type=f32
-            )
-        for s in range(4):
-            part = result[s * 128 : (s + 1) * 128]
-            current_ref[s, r] = part.astype(jnp.bfloat16)
-            base_ref[r, s] = masked[s * 128 : (s + 1) * 128] + part
-        return carry
-
-    lax.fori_loop(0, 4, row_tile, 0)
-
-
-def hop_one(slots, adj, pool):
-    vmem = pl.BlockSpec(memory_space=pltpu.VMEM)
-    return pl.pallas_call(
-        hop_one_kernel,
-        name="hop_one",
-        out_shape=(
-            jax.ShapeDtypeStruct((4, 4, 128, 128), jnp.bfloat16),
-            jax.ShapeDtypeStruct((4, 4, 128, 128), jnp.float32),
-        ),
-        in_specs=[pl.BlockSpec(memory_space=pltpu.SMEM), vmem, vmem],
-        out_specs=(vmem, vmem),
-    )(slots, adj, pool)
+        + [pltpu.VMEM((4, 72, 128), bf16)] * 14
+        + [pltpu.VMEM((4, 128, 128), bf16)] * 28
+        + marks(2)
+        + marks(4)
+        + [dma((7,)), dma((7,)), dma(())],
+        compiler_params=pltpu.CompilerParams(collective_id=1, has_side_effects=True),
+    )(own_ids, slots, own_ids[None], features, masks, adj)
 
 
 def column(row):
@@ -591,15 +617,8 @@
     weight_in, bias_in, weight_out, bias_out,
 ):
     classes = weight_out.shape[1]
-    own_ids = serve_ids.reshape(-1)
-    ids = jnp.pad(own_ids[None], ((0, 7), (0, 96)))
     slots, adj = col_slot[0], adj_blocks[0]
-    tiles = features.reshape(4, 2, 64, 128).transpose(1, 0, 2, 3)
-    masks = keep_masks.reshape(2, 2, 4, 128).transpose(0, 2, 1, 3)
-    both = jnp.concatenate([tiles, jnp.pad(masks, ((0, 0), (0, 0), (0, 6), (0, 0)))], 2)
-    pool = exchange(own_ids, ids, both, 1)
-    current, base = hop_one(slots, adj, pool)
-    pool = exchange(own_ids, ids, current, 2)
+    pool, base = spread(serve_ids.reshape(-1), slots, features[0], keep_masks[0], adj)
     grads = mlp(
         slots, adj, pool, base, node_labels.reshape(4, 128), labeled.reshape(4, 128),
         weight_in, bias_in[None], weight_out.T, bias_out[None],

time: 171 us -> 159 us (0.930)
  Pallas kernels: 166 us -> 158 us
  local copies, waits for them, and re-layouts: 2.87 us -> 0 us
    pallas_call x3 -> x1, Pallas kernels: 96.3 us -> 87.4 us  [spread(): pl.pallas_call(spread_kernel, name='spread', out_shape=(jax.ShapeDtypeStr...]
where the time goes in v2:
time: 159 us
  Pallas kernels  158 us (99%)
    pallas_call x1, Pallas kernels, spread(): pl.pallas_call(spread_kernel, name='spread', out_shape=(jax.ShapeDtypeStr...  87.4 us
    pallas_call x1, Pallas kernels, all_reduce(): pl.pallas_call(all_reduce_kernel, name='all_reduce', out_shape=jax.ShapeD...  47.6 us
    pallas_call x1, Pallas kernels, mlp(): pl.pallas_call(mlp_kernel, name='mlp', out_shape=jax.ShapeDtypeStruct((8,...  20.6 us

profile of v2, /device:TPU:1, one launch (start us, length us, event | category | flops | bytes accessed | tf_op | source)
XLA Modules:
  0.0 158.7 jit_solution(14327316615455742751)
XLA Ops:
  0.6 87.4 %spread.1 = (bf16[36,4,128,128]{3,2,1,0:T(8,128)(2,1)}, f32[4,4,128,128]{3,2,1,0:T(8,128)}) custom-call(s32[32]{0:T(128)} %bitcast.26, s32[4,10]{1,0:T(4,128)} %bitcast.22, s32[1,32]{1,0:T(1,128)} %bitcast.27, bf16[512,128]{1,0:T(8,128)(2,1)} %bitcast.21, bf16[4,512]{1,0:T(4,128)(2,1)} %bitcast.24, bf16[4,10,128,128]{3,2,1,0:T(8,128)(2,1)} %bitcast.16), custom_call_target="tpu_custom_call" | custom-call | tf_op jit(solution)/shard_map/spread/pallas_call | solution.py:452
  88.0 20.6 %mlp.1 = f32[8,320,128]{2,1,0:T(8,128)} custom-call(s32[4,10]{1,0:T(4,128)} %bitcast.23, bf16[4,10,128,128]{3,2,1,0:T(8,128)(2,1)} %bitcast.17, bf16[36,4,128,128]{3,2,1,0:T(8,128)(2,1)} %get-tuple-element.10.pool_ref, f32[4,4,128,128]{3,2,1,0:T(8,128)} %get-tuple-element.11.base_ref, s32[4,128]{1,0:T(4,128)} %bitcast.28, s32[4,128]{1,0:T(4,128)} %bitcast.29, ...), custom_call_target="tpu_custom_call" | custom-call | tf_op jit(solution)/shard_map/mlp/pallas_call | solution.py:575
  108.6 47.6 %all_reduce.1 = f32[2,2,8,5,16,128]{5,4,3,2,1,0:T(8,128)} custom-call(f32[2,2,8,5,16,128]{5,4,3,2,1,0:T(8,128)} %bitcast.18), custom_call_target="tpu_custom_call" | custom-call | tf_op jit(solution)/shard_map/all_reduce/pallas_call | solution.py:231
  156.2 2.5 %unpack.1 = (f32[128,1024]{1,0:T(8,128)}, f32[1,1024]{1,0:T(1,128)}, f32[172,1024]{1,0:T(8,128)}, f32[1,172]{1,0:T(1,128)}) custom-call(f32[8,320,128]{2,1,0:T(8,128)} %bitcast.19), custom_call_target="tpu_custom_call" | custom-call | tf_op jit(solution)/shard_map/unpack/pallas_call | solution.py:606

commit v3 on v2

--- a/solution.py
+++ b/solution.py
@@ -23,234 +23,6 @@
     z = lax.div(dom, 4)
     c = lax.rem(dom, 2)
     return x, y, z, c
-
-
-def all_reduce_kernel(
-    g_ref, o_ref, core_in, held, first_in, second, second_in, third, third_in, fourth,
-    core_s, core_r, one_s, one_r, two_s, two_r, three_s, three_r,
-    four_s, four_r, five_s, five_r, six_s, six_r,
-):
-    x, y, z, c = my_place()
-    other = lax.rem(c + 1, 2)
-    partner = place(x, y, z, other)
-    mine = (z, y)
-
-    def along(axis, d):
-        if axis == 0:
-            k = lax.rem(z + d, 8)
-            return k, place(x, y, k, c)
-        k = lax.rem(y + d, 8)
-        return k, place(x, k, z, c)
-
-    def remote(src, dst, send_sem, recv_sem, target):
-        return pltpu.make_async_remote_copy(
-            src_ref=src, dst_ref=dst, send_sem=send_sem, recv_sem=recv_sem,
-            device_id=target, device_id_type=MESH,
-        )
-
-    def each(start, stop, body):
-        def step(i, carry):
-            body(i)
-            return carry
-
-        lax.fori_loop(start, stop, step, 0)
-
-    barrier = pltpu.get_barrier_semaphore()
-    pl.semaphore_signal(barrier, inc=1, device_id=partner, device_id_type=MESH)
-
-    def greet(d):
-        for axis in range(2):
-            pl.semaphore_signal(barrier, inc=1, device_id=along(axis, d)[1], device_id_type=MESH)
-
-    def greet_x(d):
-        target = place(lax.rem(x + d, 4), y, z, c)
-        pl.semaphore_signal(barrier, inc=1, device_id=target, device_id_type=MESH)
-
-    each(1, 8, greet)
-    each(1, 4, greet_x)
-    second[...] = jnp.zeros_like(second)
-    pl.semaphore_wait(barrier, 18)
-
-    def core_copy(half, d):
-        k = lax.rem(mine[half] + d, 8)
-        return remote(
-            g_ref.at[other, half, k], core_in.at[half, k],
-            core_s.at[half, d], core_r.at[half, d], partner,
-        )
-
-    def core_start(i):
-        for half in range(2):
-            core_copy(half, lax.rem(i, 8)).start()
-
-    each(1, 9, core_start)
-
-    def one_copy(half, d):
-        k, target = along(half, d)
-        return remote(
-            held.at[half, k], first_in.at[half, d - 1],
-            one_s.at[half, d - 1], one_r.at[half, d - 1], target,
-        )
-
-    def core_add(i):
-        d = lax.rem(i, 8)
-        for half in range(2):
-            k = lax.rem(mine[half] + d, 8)
-            core_copy(half, d).wait_recv()
-            held[half, k] = g_ref[c, half, k] + core_in[half, k]
-
-    def one_step(d):
-        core_add(d)
-        for half in range(2):
-            one_copy(half, d).start()
-
-    each(1, 8, one_step)
-    core_add(8)
-
-    def one_wait(d):
-        for half in range(2):
-            one_copy(half, d).wait_recv()
-
-    each(1, 8, one_wait)
-    for half in range(2):
-        total = held[half, mine[half]]
-        for d in range(7):
-            total = total + first_in[half, d]
-        second[half, pl.ds(0, 5)] = total
-
-    def two_copy(half, d):
-        k, target = along(1 - half, d)
-        return remote(
-            second.at[half, k], second_in.at[half, d - 1],
-            two_s.at[half, d - 1], two_r.at[half, d - 1], target,
-        )
-
-    def two_step(d):
-        for half in range(2):
-            two_copy(half, d).start()
-
-    def two_wait(d):
-        for half in range(2):
-            two_copy(half, d).wait_recv()
-
-    each(1, 8, two_step)
-    each(1, 8, two_wait)
-    for half in range(2):
-        total = second[half, mine[1 - half]]
-        for d in range(7):
-            total = total + second_in[half, d]
-        third[half] = total
-
-    def three_copy(d):
-        target = place(lax.rem(x + d, 4), y, z, c)
-        return remote(third, third_in.at[x], three_s.at[d - 1], three_r.at[d - 1], target)
-
-    each(1, 4, lambda d: three_copy(d).start())
-    third_in[x] = third[...]
-    each(1, 4, lambda d: three_copy(d).wait_recv())
-    total = (third_in[0] + third_in[1]) + (third_in[2] + third_in[3])
-    for half in range(2):
-        fourth[half, mine[1 - half]] = total[half]
-
-    def four_copy(half, d):
-        target = along(1 - half, d)[1]
-        piece = fourth.at[half, mine[1 - half]]
-        return remote(piece, piece, four_s.at[half, d - 1], four_r.at[half, d - 1], target)
-
-    def four_step(d):
-        for half in range(2):
-            four_copy(half, d).start()
-
-    def four_wait(d):
-        for half in range(2):
-            four_copy(half, d).wait_recv()
-
-    each(1, 8, four_step)
-    each(1, 8, four_wait)
-
-    def five_copy(half, d):
-        target = along(half, d)[1]
-        return remote(
-            fourth.at[half, pl.ds(0, 5)], o_ref.at[c, half, mine[half]],
-            five_s.at[half, d - 1], five_r.at[half, d - 1], target,
-        )
-
-    def five_step(d):
-        for half in range(2):
-            five_copy(half, d).start()
-
-    each(1, 8, five_step)
-
-    def six_copy(half, d):
-        k = lax.rem(mine[half] + 8 - d, 8)
-        piece = o_ref.at[c, half, k]
-        return remote(piece, piece, six_s.at[half, d - 1], six_r.at[half, d - 1], partner)
-
-    def six_own(half):
-        return remote(
-            fourth.at[half, pl.ds(0, 5)], o_ref.at[c, half, mine[half]],
-            six_s.at[half, 7], six_r.at[half, 7], partner,
-        )
-
-    for half in range(2):
-        six_own(half).start()
-        o_ref[c, half, mine[half]] = fourth[half, pl.ds(0, 5)]
-
-    def six_step(d):
-        for half in range(2):
-            five_copy(half, d).wait_recv()
-            six_copy(half, d).start()
-
-    each(1, 8, six_step)
-
-    def finish(d):
-        for half in range(2):
-            one_copy(half, d).wait_send()
-            two_copy(half, d).wait_send()
-            four_copy(half, d).wait_send()
-            five_copy(half, d).wait_send()
-            six_copy(half, d).wait_send()
-            six_copy(half, d).wait_recv()
-
-    def finish_core(d):
-        for half in range(2):
-            core_copy(half, d).wait_send()
-
-    each(1, 8, finish)
-    each(0, 8, finish_core)
-    each(1, 4, lambda d: three_copy(d).wait_send())
-    for half in range(2):
-        six_own(half).wait_send()
-        six_own(half).wait_recv()
-
-
-def all_reduce(grads):
-    piece = (5, 16, 128)
-    f32 = jnp.float32
-    dma = pltpu.SemaphoreType.DMA
-    shape = (2, 2, 8) + piece
-    return pl.pallas_call(
-        all_reduce_kernel,
-        name="all_reduce",
-        out_shape=jax.ShapeDtypeStruct(shape, f32),
-        in_specs=[pl.BlockSpec(memory_space=pltpu.VMEM)],
-        out_specs=pl.BlockSpec(memory_space=pltpu.VMEM),
-        scratch_shapes=[
-            pltpu.VMEM((2, 8) + piece, f32),
-            pltpu.VMEM((2, 8) + piece, f32),
-            pltpu.VMEM((2, 7) + piece, f32),
-            pltpu.VMEM((2, 8, 16, 128), f32),
-            pltpu.VMEM((2, 7, 16, 128), f32),
-            pltpu.VMEM((2, 16, 128), f32),
-            pltpu.VMEM((4, 2, 16, 128), f32),
-            pltpu.VMEM((2, 8, 16, 128), f32),
-        ]
-        + [dma((2, 8))] * 2
-        + [dma((2, 7))] * 4
-        + [dma((3,))] * 2
-        + [dma((2, 7))] * 4
-        + [dma((2, 8))] * 2,
-        compiler_params=pltpu.CompilerParams(collective_id=0, has_side_effects=True),
-    )(grads.reshape(shape)).reshape(grads.shape)
 
 def spread_kernel(
     own_ids, slots_ref, ids_ref, feat_ref, mask_ref, adj_ref, pool_ref, base_ref,
@@ -481,14 +253,56 @@
     return jnp.broadcast_to(row, (128, 128)).T[:, :1]
 
 
-def mlp_kernel(
+def learn_kernel(
     slots_ref, adj_ref, pool_ref, base_ref, labels_ref, labeled_ref,
-    w_in_ref, b_in_ref, w_out_ref, b_out_ref, g_ref,
-    xbar, xbar_t, act, slope, dlog, dlog_t,
+    w_in_ref, b_in_ref, w_out_ref, b_out_ref, o_ref,
+    xbar, xbar_t, pre_s, act, slope, prob_s, dlog, dlog_t, dpre_s, g_ref,
+    core_in, held, first_in, second, second_in, third, third_in, fourth,
+    core_s, core_r, one_s, one_r, two_s, two_r, three_s, three_r,
+    four_s, four_r, five_s, five_r, six_s, six_r,
 ):
     f32, bf16 = jnp.float32, jnp.bfloat16
     classes = w_out_ref.shape[0]
     nt = (((1,), (1,)), ((), ()))
+    x, y, z, c = my_place()
+    other = lax.rem(c + 1, 2)
+    partner = place(x, y, z, other)
+    mine = (z, y)
+
+    def along(axis, d):
+        if axis == 0:
+            k = lax.rem(z + d, 8)
+            return k, place(x, y, k, c)
+        k = lax.rem(y + d, 8)
+        return k, place(x, k, z, c)
+
+    def remote(src, dst, send_sem, recv_sem, target):
+        return pltpu.make_async_remote_copy(
+            src_ref=src, dst_ref=dst, send_sem=send_sem, recv_sem=recv_sem,
+            device_id=target, device_id_type=MESH,
+        )
+
+    def each(start, stop, body):
+        def step(i, carry):
+            body(i)
+            return carry
+
+        lax.fori_loop(start, stop, step, 0)
+
+    barrier = pltpu.get_barrier_semaphore()
+    pl.semaphore_signal(barrier, inc=1, device_id=partner, device_id_type=MESH)
+
+    def greet(d):
+        for axis in range(2):
+            pl.semaphore_signal(barrier, inc=1, device_id=along(axis, d)[1], device_id_type=MESH)
+
+    def greet_x(d):
+        target = place(lax.rem(x + d, 4), y, z, c)
+        pl.semaphore_signal(barrier, inc=1, device_id=target, device_id_type=MESH)
+
+    each(1, 8, greet)
+    each(1, 4, greet_x)
+    second[...] = jnp.zeros_like(second)
     g_ref[...] = jnp.zeros_like(g_ref)
 
     def row_tile(r, bias_total):
@@ -507,85 +321,267 @@
             mean = (base_ref[r, s] + hop[:, s * 128 : (s + 1) * 128]) * (
                 1.0 / ((ORDER + 1) * KEEP_RATE)
             )
-            xbar[r, s * 128 : (s + 1) * 128] = mean.astype(bf16)
-            xbar_t[r, :, s * 128 : (s + 1) * 128] = mean.T.astype(bf16)
-
-        rows = xbar[r]
-        logits = jnp.zeros((512, classes), f32) + b_out_ref[...]
+            at = pl.ds(pl.multiple_of(r * 512 + s * 128, 128), 128)
+            xbar[s * 128 : (s + 1) * 128] = mean.astype(bf16)
+            xbar_t[:, at] = mean.T.astype(bf16)
+
         for h in range(4):
             cols = slice(h * 256, (h + 1) * 256)
-            pre = jnp.dot(rows, w_in_ref[:, cols], preferred_element_type=f32) + b_in_ref[:, cols]
-            sigma = 1.0 / (1.0 + jnp.exp(-pre))
-            hidden = (pre * sigma).astype(bf16)
-            act[h, r] = hidden
-            slope[h, r] = sigma * (1.0 + pre * (1.0 - sigma))
-            logits += lax.dot_general(hidden, w_out_ref[:, cols], nt, preferred_element_type=f32)
-
-        expo = jnp.exp(logits)
-        prob = expo / jnp.sum(expo, -1, keepdims=True)
-        parts = [prob[s * 128 : (s + 1) * 128] for s in range(4)]
-        average = (parts[0] + parts[1] + parts[2] + parts[3]) * 0.25
+            pre_s[h] = (
+                jnp.dot(xbar[...], w_in_ref[:, cols], preferred_element_type=f32)
+                + b_in_ref[:, cols]
+            )
+            for b in range(0, 512, 32):
+                at = pl.ds(pl.multiple_of(r * 512 + b, 32), 32)
+                pre = pre_s[h, b : b + 32]
+                sigma = 0.5 * jnp.tanh(0.5 * pre) + 0.5
+                value = pre * sigma
+                act[h, at] = value.astype(bf16)
+                slope[h, at] = sigma + value * (1.0 - sigma)
+
+        here = pl.ds(pl.multiple_of(r * 512, 512), 512)
+        hidden = jnp.concatenate([act[h, here] for h in range(4)], 1)
+        prob_s[...] = (
+            lax.dot_general(hidden, w_out_ref[...], nt, preferred_element_type=f32) + b_out_ref[...]
+        )
+        average = jnp.zeros((128, classes), f32)
+        for s in range(4):
+            expo = jnp.exp(prob_s[s * 128 : (s + 1) * 128])
+            part = expo * (1.0 / jnp.sum(expo, -1, keepdims=True))
+            prob_s[s * 128 : (s + 1) * 128] = part
+            average = average + part
+        average = average * 0.25
         squares = average * average
-        sharp = squares / jnp.sum(squares, -1, keepdims=True)
+        sharp = squares * (1.0 / jnp.sum(squares, -1, keepdims=True))
         label = column(labels_ref[pl.ds(r, 1), :].astype(f32)).astype(jnp.int32)
         used = column(labeled_ref[pl.ds(r, 1), :].astype(f32))
         onehot = (label == lax.broadcasted_iota(jnp.int32, (128, classes), 1)).astype(f32)
         for s in range(4):
-            push = 2.0 * (parts[s] - sharp)
-            inner = jnp.sum(push * parts[s], -1, keepdims=True)
-            dlogits = (used * (parts[s] - onehot) + parts[s] * (push - inner)) * (1.0 / 2048.0)
+            part = prob_s[s * 128 : (s + 1) * 128]
+            push = 2.0 * (part - sharp)
+            inner = jnp.sum(push * part, -1, keepdims=True)
+            dlogits = (used * (part - onehot) + part * (push - inner)) * (1.0 / 2048.0)
             bias_total = bias_total + jnp.sum(dlogits, 0, keepdims=True)
-            dlog[r, s * 128 : (s + 1) * 128] = dlogits.astype(bf16)
-            dlog_t[r, :, s * 128 : (s + 1) * 128] = dlogits.T.astype(bf16)
+            at = pl.ds(pl.multiple_of(r * 512 + s * 128, 128), 128)
+            dlog[at] = dlogits.astype(bf16)
+            dlog_t[:, at] = dlogits.T.astype(bf16)
         return bias_total
 
     bias_total = lax.fori_loop(0, 4, row_tile, jnp.zeros((1, classes), f32))
     g_ref[0, 301:302, :] = bias_total[:, :128]
     g_ref[1, 301:302, : classes - 128] = bias_total[:, 128:]
 
-    for h in range(4):
-        cols = slice(h * 256, (h + 1) * 256)
-
-        def back(r, carry):
-            w_in_grad, w_out_grad, b_in_grad = carry
-            dact = jnp.dot(dlog[r], w_out_ref[:, cols], preferred_element_type=f32)
-            dpre = dact * slope[h, r]
-            w_in_grad = w_in_grad + jnp.dot(
-                xbar_t[r], dpre.astype(bf16), preferred_element_type=f32
-            )
-            w_out_grad = w_out_grad + jnp.dot(dlog_t[r], act[h, r], preferred_element_type=f32)
-            b_in_grad = b_in_grad + jnp.sum(dpre, 0, keepdims=True)
-            return w_in_grad, w_out_grad, b_in_grad
-
-        w_in_grad, w_out_grad, b_in_grad = lax.fori_loop(
-            0, 4, back,
-            (jnp.zeros((128, 256), f32), jnp.zeros((classes, 256), f32), jnp.zeros((1, 256), f32)),
-        )
+    def chunk(h):
+        cols = pl.ds(pl.multiple_of(h * 256, 256), 256)
+
+        def back(r, total):
+            here = pl.ds(pl.multiple_of(r * 512, 512), 512)
+            dact = jnp.dot(dlog[here], w_out_ref[:, cols], preferred_element_type=f32)
+            dpre = dact * slope[h, here]
+            dpre_s[here] = dpre.astype(bf16)
+            return total + jnp.sum(dpre.reshape(64, 8, 256), 0)
+
+        total = lax.fori_loop(0, 4, back, jnp.zeros((8, 256), f32))
+        b_in_grad = jnp.sum(total, 0, keepdims=True)
+        w_in_grad = jnp.dot(xbar_t[...], dpre_s[...], preferred_element_type=f32)
+        w_out_grad = jnp.dot(dlog_t[...], act[h], preferred_element_type=f32)
         for i in range(2):
             lanes = slice(i * 128, (i + 1) * 128)
             g_ref[2 * h + i, :128] = w_in_grad[:, lanes]
             g_ref[2 * h + i, 128 : 128 + classes] = w_out_grad[:, lanes]
             g_ref[2 * h + i, 300:301] = b_in_grad[:, lanes]
 
-
-def mlp(slots, adj, pool, base, labels, labeled, w_in, b_in, w_out_t, b_out):
+    def piece_at(core, half, k):
+        row = pl.ds(pl.multiple_of(lax.rem(k, 4) * 80, 16), 80)
+        return core * 4 + half * 2 + lax.div(k, 4), row
+
+    def core_copy(half, d):
+        k = lax.rem(mine[half] + d, 8)
+        return remote(
+            g_ref.at[piece_at(other, half, k)], core_in.at[half, k],
+            core_s.at[half, d], core_r.at[half, d], partner,
+        )
+
+    for half in range(2):
+        chunk(other * 2 + half)
+        if half == 0:
+            pl.semaphore_wait(barrier, 18)
+        each(1, 9, lambda i: core_copy(half, lax.rem(i, 8)).start())
+
+    def one_copy(half, d):
+        k, target = along(half, d)
+        return remote(
+            held.at[half, k], first_in.at[half, d - 1],
+            one_s.at[half, d - 1], one_r.at[half, d - 1], target,
+        )
+
+    for half in range(2):
+        chunk(c * 2 + half)
+
+        def core_add(i):
+            d = lax.rem(i, 8)
+            k = lax.rem(mine[half] + d, 8)
+            core_copy(half, d).wait_recv()
+            held[half, k] = (g_ref[piece_at(c, half, k)] + core_in[half, k]).reshape(5, 16, 128)
+
+        def one_step(d):
+            core_add(d)
+            one_copy(half, d).start()
+
+        each(1, 8, one_step)
+        core_add(8)
+
+    for half in range(2):
+        each(1, 8, lambda d: one_copy(half, d).wait_recv())
+        total = held[half, mine[half]]
+        for d in range(7):
+            total = total + first_in[half, d]
+        second[half, pl.ds(0, 5)] = total
+
+    def two_copy(half, d):
+        k, target = along(1 - half, d)
+        return remote(
+            second.at[half, k], second_in.at[half, d - 1],
+            two_s.at[half, d - 1], two_r.at[half, d - 1], target,
+        )
+
+    def two_step(d):
+        for half in range(2):
+            two_copy(half, d).start()
+
+    def two_wait(d):
+        for half in range(2):
+            two_copy(half, d).wait_recv()
+
+    each(1, 8, two_step)
+    each(1, 8, two_wait)
+    for half in range(2):
+        total = second[half, mine[1 - half]]
+        for d in range(7):
+            total = total + second_in[half, d]
+        third[half] = total
+
+    def three_copy(d):
+        target = place(lax.rem(x + d, 4), y, z, c)
+        return remote(third, third_in.at[x], three_s.at[d - 1], three_r.at[d - 1], target)
+
+    each(1, 4, lambda d: three_copy(d).start())
+    third_in[x] = third[...]
+    each(1, 4, lambda d: three_copy(d).wait_recv())
+    total = (third_in[0] + third_in[1]) + (third_in[2] + third_in[3])
+    for half in range(2):
+        fourth[half, mine[1 - half]] = total[half]
+
+    def four_copy(half, d):
+        target = along(1 - half, d)[1]
+        piece = fourth.at[half, mine[1 - half]]
+        return remote(piece, piece, four_s.at[half, d - 1], four_r.at[half, d - 1], target)
+
+    def four_step(d):
+        for half in range(2):
+            four_copy(half, d).start()
+
+    def four_wait(d):
+        for half in range(2):
+            four_copy(half, d).wait_recv()
+
+    each(1, 8, four_step)
+    each(1, 8, four_wait)
+
+    def five_copy(half, d):
+        target = along(half, d)[1]
+        return remote(
+            fourth.at[half, pl.ds(0, 5)], o_ref.at[c, half, mine[half]],
+            five_s.at[half, d - 1], five_r.at[half, d - 1], target,
+        )
+
+    def five_step(d):
+        for half in range(2):
+            five_copy(half, d).start()
+
+    each(1, 8, five_step)
+
+    def six_copy(half, d):
+        k = lax.rem(mine[half] + 8 - d, 8)
+        piece = o_ref.at[c, half, k]
+        return remote(piece, piece, six_s.at[half, d - 1], six_r.at[half, d - 1], partner)
+
+    def six_own(half):
+        return remote(
+            fourth.at[half, pl.ds(0, 5)], o_ref.at[c, half, mine[half]],
+            six_s.at[half, 7], six_r.at[half, 7], partner,
+        )
+
+    for half in range(2):
+        six_own(half).start()
+        o_ref[c, half, mine[half]] = fourth[half, pl.ds(0, 5)]
+
+    def six_step(d):
+        for half in range(2):
+            five_copy(half, d).wait_recv()
+            six_copy(half, d).start()
+
+    each(1, 8, six_step)
+
+    def finish(d):
+        for half in range(2):
+            one_copy(half, d).wait_send()
+            two_copy(half, d).wait_send()
+            four_copy(half, d).wait_send()
+            five_copy(half, d).wait_send()
+            six_copy(half, d).wait_send()
+            six_copy(half, d).wait_recv()
+
+    def finish_core(d):
+        for half in range(2):
+            core_copy(half, d).wait_send()
+
+    each(1, 8, finish)
+    each(0, 8, finish_core)
+    each(1, 4, lambda d: three_copy(d).wait_send())
+    for half in range(2):
+        six_own(half).wait_send()
+        six_own(half).wait_recv()
+
+
+def learn(slots, adj, pool, base, labels, labeled, w_in, b_in, w_out_t, b_out):
     vmem = pl.BlockSpec(memory_space=pltpu.VMEM)
     classes = w_out_t.shape[0]
-    bf16 = jnp.bfloat16
+    bf16, f32 = jnp.bfloat16, jnp.float32
+    piece = (5, 16, 128)
+    dma = pltpu.SemaphoreType.DMA
     return pl.pallas_call(
-        mlp_kernel,
-        name="mlp",
-        out_shape=jax.ShapeDtypeStruct((8, GROWS, 128), jnp.float32),
+        learn_kernel,
+        name="learn",
+        out_shape=jax.ShapeDtypeStruct((2, 2, 8) + piece, f32),
         in_specs=[pl.BlockSpec(memory_space=pltpu.SMEM)] + [vmem] * 9,
         out_specs=vmem,
         scratch_shapes=[
-            pltpu.VMEM((4, 512, 128), bf16),
-            pltpu.VMEM((4, 128, 512), bf16),
-            pltpu.VMEM((4, 4, 512, 256), bf16),
-            pltpu.VMEM((4, 4, 512, 256), jnp.float32),
-            pltpu.VMEM((4, 512, classes), bf16),
-            pltpu.VMEM((4, classes, 512), bf16),
-        ],
+            pltpu.VMEM((512, 128), bf16),
+            pltpu.VMEM((128, 2048), bf16),
+            pltpu.VMEM((4, 512, 256), f32),
+            pltpu.VMEM((4, 2048, 256), bf16),
+            pltpu.VMEM((4, 2048, 256), f32),
+            pltpu.VMEM((512, classes), f32),
+            pltpu.VMEM((2048, classes), bf16),
+            pltpu.VMEM((classes, 2048), bf16),
+            pltpu.VMEM((2048, 256), bf16),
+            pltpu.VMEM((8, GROWS, 128), f32),
+            pltpu.VMEM((2, 8, 80, 128), f32),
+            pltpu.VMEM((2, 8) + piece, f32),
+            pltpu.VMEM((2, 7) + piece, f32),
+            pltpu.VMEM((2, 8, 16, 128), f32),
+            pltpu.VMEM((2, 7, 16, 128), f32),
+            pltpu.VMEM((2, 16, 128), f32),
+            pltpu.VMEM((4, 2, 16, 128), f32),
+            pltpu.VMEM((2, 8, 16, 128), f32),
+        ]
+        + [dma((2, 8))] * 2
+        + [dma((2, 7))] * 4
+        + [dma((3,))] * 2
+        + [dma((2, 7))] * 4
+        + [dma((2, 8))] * 2,
+        compiler_params=pltpu.CompilerParams(collective_id=0, has_side_effects=True),
     )(slots, adj, pool, base, labels, labeled, w_in, b_in, w_out_t, b_out)
 
 
@@ -619,11 +615,11 @@
     classes = weight_out.shape[1]
     slots, adj = col_slot[0], adj_blocks[0]
     pool, base = spread(serve_ids.reshape(-1), slots, features[0], keep_masks[0], adj)
-    grads = mlp(
+    summed = learn(
         slots, adj, pool, base, node_labels.reshape(4, 128), labeled.reshape(4, 128),
         weight_in, bias_in[None], weight_out.T, bias_out[None],
     )
-    w_in, b_in, w_out_t, b_out = unpack(all_reduce(grads), classes)
+    w_in, b_in, w_out_t, b_out = unpack(summed.reshape(8, GROWS, 128), classes)
     return (w_in, b_in[0], w_out_t.T, b_out[0])
 
 

time: 159 us -> 153 us (0.962)
  Pallas kernels: 158 us -> 152 us
    pallas_call x2 -> x1, Pallas kernels: 68.1 us -> 62.4 us  [learn(): pl.pallas_call(learn_kernel, name='learn', out_shape=jax.ShapeDtypeStruct...]
where the time goes in v3:
time: 153 us
  Pallas kernels  152 us (99%)
    pallas_call x1, Pallas kernels, spread(): pl.pallas_call(spread_kernel, name='spread', out_shape=(jax.ShapeDtypeStr...  87.4 us
    pallas_call x1, Pallas kernels, learn(): pl.pallas_call(learn_kernel, name='learn', out_shape=jax.ShapeDtypeStruct...  62.4 us

profile of v3, /device:TPU:1, one launch (start us, length us, event | category | flops | bytes accessed | tf_op | source)
XLA Modules:
  0.0 152.9 jit_solution(5340560795487859241)
XLA Ops:
  0.6 87.4 %spread.1 = (bf16[36,4,128,128]{3,2,1,0:T(8,128)(2,1)}, f32[4,4,128,128]{3,2,1,0:T(8,128)}) custom-call(s32[32]{0:T(128)} %bitcast.24, s32[4,10]{1,0:T(4,128)} %bitcast.20, s32[1,32]{1,0:T(1,128)} %bitcast.25, bf16[512,128]{1,0:T(8,128)(2,1)} %bitcast.19, bf16[4,512]{1,0:T(4,128)(2,1)} %bitcast.22, bf16[4,10,128,128]{3,2,1,0:T(8,128)(2,1)} %bitcast.15), custom_call_target="tpu_custom_call" | custom-call | tf_op jit(solution)/shard_map/spread/pallas_call | solution.py:224
  88.0 62.4 %learn.1 = f32[2,2,8,5,16,128]{5,4,3,2,1,0:T(8,128)} custom-call(s32[4,10]{1,0:T(4,128)} %bitcast.21, bf16[4,10,128,128]{3,2,1,0:T(8,128)(2,1)} %bitcast.16, bf16[36,4,128,128]{3,2,1,0:T(8,128)(2,1)} %get-tuple-element.10.pool_ref, f32[4,4,128,128]{3,2,1,0:T(8,128)} %get-tuple-element.11.base_ref, s32[4,128]{1,0:T(4,128)} %bitcast.26, s32[4,128]{1,0:T(4,128)} %bitcast.27, ...), custom_call_target="tpu_custom_call" | custom-call | tf_op jit(solution)/shard_map/learn/pallas_call | solution.py:553
  150.4 2.5 %unpack.1 = (f32[128,1024]{1,0:T(8,128)}, f32[1,1024]{1,0:T(1,128)}, f32[172,1024]{1,0:T(8,128)}, f32[1,172]{1,0:T(1,128)}) custom-call(f32[8,320,128]{2,1,0:T(8,128)} %bitcast.17), custom_call_target="tpu_custom_call" | custom-call | tf_op jit(solution)/shard_map/unpack/pallas_call | solution.py:602
